TPU v7x, 512 devices: a whole 4x4x16 slice. The times are simulated.
512 devices in a mesh: row: 32 (over z, core), col: 16 (over x, y).
Axes of the slice: x: 4, y: 4, z: 16, core: 2. Of those that a mesh axis runs over, the one named last changes fastest.
Arguments:
- front_entries: float32 [16384, 16384], P('row', 'col'), may hold values from 0 to 3, as said below
- tile_group: int32 [32], replicated, may hold values from 0 to 3
- child_factor: bfloat16 [16384, 256], P('row', 'col'), may hold values from -0.375 to 0.375
- row_map: int32 [128], replicated, may hold values from 0 to 127, as said below
Outputs:
- factor_panels: bfloat16 [16384, 512], P('row', 'col')
- schur_block: float32 [16384, 16384], P('row', 'col')
Inputs may be any that keep to these rules, and one draw needn't show every extreme that they name: `front_entries`: Symmetric; assembled is positive definite. `row_map`: A permutation of the parent tiles. The tile in row block r (blocks of 512 rows) goes to a parent tile in row block r or in the row block whose index differs from r in the highest bit.
All inputs are finite; a program needn't handle non-finite values.
Results may differ from a plain program's by a relative error of at most 0.0026.
Values may be sent and summed in bfloat16 or wider, within the bound.
A program may use at most 64 MiB of HBM per device.

v0:
```python
import jax
import jax.numpy as jnp
from jax import lax
from jax.sharding import PartitionSpec as P

PW = 256
NP = 2
TS = 128
MT = 512


def swapped(value, axis, stride):
    mask = 2**stride
    pairs = [(source, source ^ mask) for source in range(lax.axis_size(axis))]
    return lax.ppermute(value, axis, pairs)


def broadcast(value, axis, source):
    kept = jnp.where(lax.axis_index(axis) == source, value, 0).astype(value.dtype)
    return lax.psum(kept, axis)


def panel_columns(matrix, offset, width_cols, fan_ratio, block_rows):
    return jnp.concatenate(
        [
            matrix[:, q * block_rows + offset : q * block_rows + offset + width_cols]
            for q in range(fan_ratio)
        ],
        axis=1,
    )


def outer_rows(left, right):
    return jnp.einsum("ik,jk->ij", left, right, preferred_element_type=jnp.float32)


def subtract_block(matrix, lead_rows, owner, low, col_from, col_to, base_col):
    region = matrix[low:, base_col + col_from : base_col + col_to]
    return matrix.at[low:, base_col + col_from : base_col + col_to].set(
        region - outer_rows(lead_rows, owner[col_from:col_to])
    )


def right_solve(lower_factor, strip):
    return lax.linalg.triangular_solve(
        lower_factor, strip, left_side=False, lower=True, transpose_a=True
    )


def local(front_entries, tile_group, child_factor, row_map):
    row_count = lax.axis_size("row")
    col_count = lax.axis_size("col")
    fan_ratio = row_count // col_count
    local_rows = front_entries.shape[0]
    local_cols = front_entries.shape[1]
    my_row = lax.axis_index("row")
    my_col = lax.axis_index("col")
    row_tiles = local_rows // MT
    col_tiles = local_cols // MT
    group_rows = lax.dynamic_slice_in_dim(tile_group, my_row * row_tiles, row_tiles)
    group_cols = lax.dynamic_slice_in_dim(tile_group, my_col * col_tiles, col_tiles)
    same_group = (group_rows[:, None] == group_cols[None, :]).astype(jnp.float32)
    masked = (
        front_entries.reshape(row_tiles, MT, col_tiles, MT) * same_group[:, None, :, None]
    ).reshape(local_rows, local_cols)
    child_full = lax.all_gather(child_factor, "col", axis=1, tiled=True)
    child_width = child_full.shape[1]
    partner_full = swapped(child_full, "row", row_count.bit_length() - 2)
    tile_count = local_rows // TS
    partner_row = jnp.bitwise_xor(my_row, row_count // 2)
    own_map = lax.dynamic_slice_in_dim(row_map, my_row * tile_count, tile_count)
    partner_map = lax.dynamic_slice_in_dim(row_map, partner_row * tile_count, tile_count)
    slot_ids = my_row * tile_count + jnp.arange(tile_count, dtype=jnp.int32)

    def place_tiles(tile_map, source):
        chooser = (tile_map[None, :] == slot_ids[:, None]).astype(jnp.bfloat16)
        placed = jnp.dot(
            chooser,
            source.reshape(tile_count, TS * child_width),
            preferred_element_type=jnp.float32,
        )
        return placed.astype(jnp.bfloat16).reshape(local_rows, child_width)

    own_parent = place_tiles(own_map, child_full)
    partner_parent = place_tiles(partner_map, partner_full)
    lower_half = my_row < row_count // 2
    child_wide = jnp.where(
        lower_half,
        jnp.concatenate([own_parent, partner_parent], axis=1),
        jnp.concatenate([partner_parent, own_parent], axis=1),
    )
    child_owners = [broadcast(child_wide, "row", fan_ratio * my_col + q) for q in range(fan_ratio)]
    matrix = jnp.concatenate(
        [
            masked[:, q * local_rows : (q + 1) * local_rows]
            + outer_rows(child_wide, child_owners[q])
            for q in range(fan_ratio)
        ],
        axis=1,
    )
    row_share = PW // row_count
    col_share = PW // col_count
    local_ids = jnp.arange(local_rows)
    coming = None
    outputs = []
    for k in range(NP):
        offset = k * row_share
        panel_strip = panel_columns(matrix, offset, row_share, fan_ratio, local_rows)
        corner = panel_strip[offset : offset + row_share]
        gathered = lax.all_gather(corner, ("row", "col"), axis=0, tiled=True)
        diagonal = (
            gathered.reshape(row_count, col_count, row_share, col_share)
            .transpose(0, 2, 1, 3)
            .reshape(PW, PW)
        )
        lower_factor = jnp.linalg.cholesky(diagonal)
        whole_strip = lax.all_gather(panel_strip, "col", axis=1, tiled=True)
        rounded = right_solve(lower_factor, whole_strip).astype(jnp.bfloat16)
        own_lower = lax.dynamic_slice_in_dim(lower_factor, my_row * row_share, row_share).astype(
            jnp.bfloat16
        )
        rounded = jnp.where((local_ids < offset)[:, None], jnp.zeros_like(rounded), rounded)
        rounded = rounded.at[offset : offset + row_share].set(own_lower)
        outputs.append(lax.dynamic_slice_in_dim(rounded, my_col * col_share, col_share, 1))
        owners = [broadcast(rounded, "row", fan_ratio * my_col + q) for q in range(fan_ratio)]
        low = offset + row_share
        lead_rows = rounded[low:]
        for q in range(fan_ratio):
            matrix = subtract_block(
                matrix, lead_rows, owners[q], low, low, local_rows, q * local_rows
            )
    pivot_done = NP * row_share
    row_keep = local_ids >= pivot_done
    col_keep = jnp.arange(local_cols) % local_rows >= pivot_done
    schur_block = jnp.where(row_keep[:, None] & col_keep[None, :], matrix, jnp.zeros_like(matrix))
    factor_panels = jnp.concatenate(outputs, axis=1)
    return (factor_panels, schur_block)


def solution(mesh):
    placed = (P("row", "col"), P(), P("row", "col"), P())
    return jax.shard_map(
        local,
        mesh=mesh,
        in_specs=placed,
        out_specs=(P("row", "col"), P("row", "col")),
        check_vma=False,
    )
```

profile of v0, /device:TPU:6, one launch (start us, length us, event | category | flops | bytes accessed | tf_op | source)
XLA Modules:
  0.0 1301.2 jit_solution(17513636110733798873)
XLA Ops:
  7.2 26.6 %all_gather.15 = bf16[512,256]{0,1:T(8,128)(2,1)S(1)} all-gather(bf16[512,16]{0,1:T(8,128)(2,1)} %param.21), channel_id=1, replica_groups=mesh['row'=32,'col'=16] {'col'}, dimensions={1}, use_global_device_ids=true | all-gather | bytes 278528 | tf_op jit(solution)/shard_map/all_gather | solution.py:66
  33.8 12.8 collective-permute-start
  47.0 0.8 fusion.44
  49.0 0.7 compare_convert_fusion
  49.8 1.9 copy.30
  51.7 3.4 collective-permute-done
  56.0 1.3 broadcast_select_fusion.1
  57.3 1.5 broadcast_multiply_fusion
  58.9 217.6 %all-reduce.12.cloned.1.call-done = (bf16[512,512]{1,0:T(8,128)(2,1)}, bf16[512,512]{1,0:T(8,128)(2,1)}) async-done(((bf16[512,512]{1,0:T(8,128)(2,1)}, bf16[512,512]{1,0:T(8,128)(2,1)}), (bf16[512,512]{1,0:T(8,128)(2,1)}, bf16[512,512]{1,0:T(8,128)(2,1)})) %all-reduce.12.cloned.1.call-update) | async-done | bytes 1048592 | tf_op jit(solution)/shard_map/psum | solution.py:20
  276.5 2.1 convolution_add_fusion.1
  279.1 1.0 copy-done.1
  280.1 196.9 %all_gather.16 = f32[4096,16]{1,0:T(8,128)S(1)} all-gather(f32[8,16]{1,0:T(8,128)S(1)} %copy.33), channel_id=1, replica_groups=mesh['row'=32,'col'=16] {'row','col'}, dimensions={0}, use_global_device_ids=true | all-gather | bytes 262656 | tf_op jit(solution)/shard_map/all_gather | solution.py:110
  477.4 0.9 reshape.255
  478.6 11.7 cholesky.130
  490.3 9.8 custom-call.13
  500.6 11.9 cholesky.147
  515.2 3.8 while.10
  515.8 1.3 bitcast_dynamic-update-slice_fusion.4
  517.7 1.3 bitcast_dynamic-update-slice_fusion.4
  519.0 19.7 %custom-call.14 = f32[2,128,128]{1,2,0:T(8,128)S(1)} custom-call(f32[2,128,128]{2,1,0:T(8,128)S(1)} %get-tuple-element.90), custom_call_target="InvertDiagBlocksLowerTriangular" | custom-call | tf_op jit(solution)/shard_map/triangular_solve/custom-call.0 | solution.py:45
  538.7 22.7 %all_gather.17 = f32[512,256]{0,1:T(8,128)S(1)} all-gather(f32[512,16]{0,1:T(8,128)S(1)} %pad_maximum_fusion.1), channel_id=1, replica_groups=mesh['row'=32,'col'=16] {'col'}, dimensions={1}, use_global_device_ids=true | all-gather | bytes 557056 | tf_op jit(solution)/shard_map/all_gather | solution.py:117
  563.2 0.8 broadcast_select_fusion.3
  564.1 1.4 pad_maximum_fusion
  565.5 203.6 %all-reduce.10.cloned.1.call-done = (bf16[512,256]{0,1:T(8,128)(2,1)}, bf16[512,256]{0,1:T(8,128)(2,1)}) async-done(((bf16[512,256]{0,1:T(8,128)(2,1)}, bf16[512,256]{0,1:T(8,128)(2,1)}), (bf16[512,256]{0,1:T(8,128)(2,1)}, bf16[512,256]{0,1:T(8,128)(2,1)})) %all-reduce.10.cloned.1.call-update) | async-done | bytes 524304 | tf_op jit(solution)/shard_map/psum | solution.py:20
  769.1 2.6 convolution_subtract_fusion.1
  771.7 5.4 scatter.21
  777.1 1.6 convolution_subtract_fusion
  778.7 3.4 scatter.24
  782.3 196.7 %all_gather.18 = f32[4096,16]{1,0:T(8,128)S(1)} all-gather(f32[8,16]{1,0:T(8,128)S(1)} %copy.38), channel_id=1, replica_groups=mesh['row'=32,'col'=16] {'row','col'}, dimensions={0}, use_global_device_ids=true | all-gather | bytes 262656 | tf_op jit(solution)/shard_map/all_gather | solution.py:110
  979.0 1.7 copy.39
  980.7 2.8 reshape.257
  983.7 11.7 cholesky.164
  995.5 9.8 custom-call.15
  1005.8 11.7 cholesky.181
  1017.5 0.6 compare_reduce_fusion
  1020.2 4.0 while.11
  1020.8 1.4 bitcast_dynamic-update-slice_fusion.5
  1022.8 1.4 bitcast_dynamic-update-slice_fusion.5
  1024.2 19.8 %custom-call.16 = f32[2,128,128]{1,2,0:T(8,128)S(1)} custom-call(f32[2,128,128]{2,1,0:T(8,128)S(1)} %get-tuple-element.91), custom_call_target="InvertDiagBlocksLowerTriangular" | custom-call | tf_op jit(solution)/shard_map/triangular_solve/custom-call.0 | solution.py:45
  1044.0 22.7 %all_gather.19 = f32[512,256]{0,1:T(8,128)S(1)} all-gather(f32[512,16]{0,1:T(8,128)S(1)} %pad_maximum_fusion.2), channel_id=1, replica_groups=mesh['row'=32,'col'=16] {'col'}, dimensions={1}, use_global_device_ids=true | all-gather | bytes 557056 | tf_op jit(solution)/shard_map/all_gather | solution.py:117
  1068.8 0.8 broadcast_select_fusion.2
  1070.3 204.5 %all-reduce.8.cloned.1.call-done = (bf16[512,256]{0,1:T(8,128)(2,1)}, bf16[512,256]{0,1:T(8,128)(2,1)}) async-done(((bf16[512,256]{0,1:T(8,128)(2,1)}, bf16[512,256]{0,1:T(8,128)(2,1)}), (bf16[512,256]{0,1:T(8,128)(2,1)}, bf16[512,256]{0,1:T(8,128)(2,1)})) %all-reduce.8.cloned.1.call-update) | async-done | bytes 524304 | tf_op jit(solution)/shard_map/psum | solution.py:20
  1274.8 2.6 convolution_subtract_fusion.3
  1277.4 5.4 scatter.26
  1282.8 1.6 convolution_subtract_fusion.2
  1284.4 5.6 scatter.29
  1290.0 1.6 and_select_fusion
  1291.6 2.9 copy.45
  (94 shorter events, 13.9 us)
Async XLA Ops:
  7.2 41.2 %copy-start.5 = (s32[32]{0:T(128)S(1)}, s32[32]{0:T(128)}, u32[]{:S(2)}) copy-start(s32[32]{0:T(128)} %param.20) | copy-start | bytes 388
  7.2 269.3 %all-reduce.12.cloned.1.call-start = ((), (), s32[]{:S(2)}) async-start(), calls=%async_computation.2 | async-start | bytes 2097152 | tf_op jit(solution)/shard_map/psum | solution.py:20
  33.8 21.3 %collective-permute-start = (bf16[512,256]{0,1:T(8,128)(2,1)S(1)}, bf16[512,256]{0,1:T(8,128)(2,1)S(1)}, u32[]{:S(2)}, u32[]{:S(2)}) collective-permute-start(bf16[512,256]{0,1:T(8,128)(2,1)S(1)} %all_gather.15), channel_id=1, source_target_pairs={{0,256},{16,272},{32,288},{48,304},{64,320},{80,336},{96,352},{112... | collective-permute-start | bytes 786440 | tf_op jit(solution)/shard_map/ppermute | solution.py:15
  56.0 2.9 copy-start.2
  57.3 711.8 %all-reduce.10.cloned.1.call-start = ((), (), s32[]{:S(2)}) async-start(), calls=%async_computation.1 | async-start | bytes 1048576 | tf_op jit(solution)/shard_map/psum | solution.py:20
  58.9 219.7 %copy-start = (f32[512,1024]{0,1:T(8,128)S(1)}, f32[512,1024]{0,1:T(8,128)}, u32[]{:S(2)}) copy-start(f32[512,1024]{0,1:T(8,128)} %broadcast_multiply_fusion) | copy-start | bytes 6291460
  276.5 2.1 copy-start.3
  276.5 2.1 copy-start.6
  279.1 1.0 copy-start.1
  564.0 710.7 %all-reduce.8.cloned.1.call-start = ((), (), s32[]{:S(2)}) async-start(), calls=%async_computation | async-start | bytes 1048576 | tf_op jit(solution)/shard_map/psum | solution.py:20
  1274.8 8.0 copy-start.4
Sparse Core Ops, SparseCore 0:
  57.4 219.0 all-reduce.11
  564.1 204.9 all-reduce.9
  1069.8 204.9 all-reduce.7
where the time goes:
time: 1310 us; the launch traced here: 1300 us
  waiting for transfers between devices  629 us (48%)
  blocking collectives  466 us (36%)
  other arithmetic  119 us (9%)
  local copies, waits for them, and re-layouts  42.6 us (3%)
  between operations  17 us (1%)
  matrix products  15 us (1%)
    psum x3, waiting for transfers between devices, broadcast(): return lax.psum(kept, axis)  626 us
    all_gather x2, blocking collectives, local(): gathered = lax.all_gather(corner, ('row', 'col'), axis=0, tiled=True)  394 us
    another operation x14, other arithmetic, local(): lower_factor = jnp.linalg.cholesky(diagonal)  69.3 us
    all_gather x2, blocking collectives, local(): whole_strip = lax.all_gather(panel_strip, 'col', axis=1, tiled=True)  45.5 us
    another operation x5, other arithmetic, right_solve(): lax.linalg.triangular_solve(lower_factor, strip, left_side=False, lower=T...  39.6 us
    all_gather x1, blocking collectives, local(): child_full = lax.all_gather(child_factor, 'col', axis=1, tiled=True)  26.6 us
  transfers between devices with their start and end apart: 4, of which 4 were waited for; matrix products, arithmetic and copies ran while one was open for 1% of the time, Pallas kernels for 0%

commit v1 on v0

v1 whole, which is shorter than its diff:
```python
import functools

import jax
import jax.numpy as jnp
from jax import lax
from jax.experimental import pallas as pl
from jax.experimental.pallas import tpu as pltpu
from jax.sharding import PartitionSpec as P

PW = 256
NP = 2
TS = 128
MT = 512
NB = 32
SUB = 8
F32 = jnp.float32
BF16 = jnp.bfloat16
MESH = pl.DeviceIdType.MESH


def loop(count, body):
    def step(i, carry):
        body(i)
        return carry

    lax.fori_loop(0, count, step, 0)


def comm_kernel(
    zin, srow, scol, child, pick,
    diag, vpiv, strip_r, strip_c, v_r, v_c,
    zbuf, partner, placed, dpiece, vpiece,
    z_s, z_r, p_s, p_r, t_s, t_r,
    plane_s, plane_r, ring_s, ring_r, sib_s, sib_r,
):
    r = lax.axis_index("row")
    c = lax.axis_index("col")
    rows = lax.axis_size("row")
    cols = lax.axis_size("col")
    z = r // 2
    core = r % 2
    chips = rows // 2
    t_row = 2 * c + core
    t_col = z
    t_self = jnp.logical_and(t_row == r, t_col == c)

    barrier = pltpu.get_barrier_semaphore()

    def hello_row(i):
        pl.semaphore_signal(barrier, inc=1, device_id=(lax.rem(r + i + 1, rows), c), device_id_type=MESH)

    def hello_col(i):
        pl.semaphore_signal(barrier, inc=1, device_id=(r, lax.rem(c + i + 1, cols)), device_id_type=MESH)

    loop(rows - 1, hello_row)
    loop(cols - 1, hello_col)

    @pl.when(jnp.logical_not(t_self))
    def _():
        pl.semaphore_signal(barrier, inc=1, device_id=(t_row, t_col), device_id_type=MESH)

    pl.semaphore_wait(barrier, rows + cols - 2 + jnp.where(t_self, 0, 1))

    def partner_copy():
        return pltpu.make_async_remote_copy(
            src_ref=child, dst_ref=partner, send_sem=p_s, recv_sem=p_r,
            device_id=(lax.rem(r + rows // 2, rows), c), device_id_type=MESH)

    def z_copy(i):
        return pltpu.make_async_remote_copy(
            src_ref=zin, dst_ref=zbuf.at[r], send_sem=z_s.at[i], recv_sem=z_r.at[i],
            device_id=(lax.rem(r + i + 1, rows), c), device_id_type=MESH)

    loop(rows - 1, lambda i: z_copy(i).start())
    partner_copy().start()
    zbuf[pl.ds(r, 1)] = zin[...][None]

    own8 = pl.ds(pl.multiple_of(r * 8, 8), 8)
    own16 = pl.ds(pl.multiple_of(c * 16, 16), 16)
    strip_c[:, own8, :] = scol[...]
    strip_r[:, own16, :] = srow[...]

    def plane_copy(a, src, dst, i):
        return pltpu.make_async_remote_copy(
            src_ref=src, dst_ref=dst, send_sem=plane_s.at[a, i], recv_sem=plane_r.at[a, i],
            device_id=(r, lax.rem(c + i + 1, cols)), device_id_type=MESH)

    def sr_copy(i):
        return plane_copy(0, srow, strip_r.at[:, own16, :], i)

    def d_copy(i):
        return plane_copy(1, dpiece, diag.at[:, own16, :], i)

    def vp_copy(i):
        return plane_copy(2, vpiece, vpiv.at[:, own16, :], i)

    def vr_copy(i):
        return plane_copy(3, placed, v_r.at[own16, :], i)

    loop(rows - 1, lambda i: z_copy(i).wait_recv())
    turned = jnp.transpose(zbuf[...].reshape(rows * 8, 128))
    dpiece[0] = turned[0:16]
    dpiece[1] = turned[16:32]
    dpiece[2] = turned[32:48]
    half = rows * 4

    def swapped_halves(x):
        return jnp.concatenate([x[:, half:], x[:, :half]], axis=1)

    vpiece[0] = (turned[64:80] + swapped_halves(turned[80:96])).astype(BF16)
    vpiece[1] = (turned[96:112] + swapped_halves(turned[112:128])).astype(BF16)
    diag[:, own16, :] = dpiece[...]
    vpiv[:, own16, :] = vpiece[...]
    loop(cols - 1, lambda i: d_copy(i).start())
    loop(cols - 1, lambda i: vp_copy(i).start())
    loop(cols - 1, lambda i: sr_copy(i).start())

    partner_copy().wait_recv()
    for j in range(MT // TS):
        total = jnp.zeros((16, TS), F32)
        for t in range(4):
            total = total + child[t].astype(F32) * pick[8 * j + t : 8 * j + t + 1, :]
            total = total + partner[t].astype(F32) * pick[8 * j + 4 + t : 8 * j + 5 + t, :]
        placed[:, j * TS : (j + 1) * TS] = total.astype(BF16)
    v_r[own16, :] = placed[...]

    def t_copy():
        return pltpu.make_async_remote_copy(
            src_ref=placed, dst_ref=v_c.at[t_row], send_sem=t_s, recv_sem=t_r,
            device_id=(t_row, t_col), device_id_type=MESH)

    @pl.when(t_self)
    def _():
        v_c[pl.ds(r, 1)] = placed[...][None]

    @pl.when(jnp.logical_not(t_self))
    def _():
        t_copy().start()

    loop(cols - 1, lambda i: vr_copy(i).start())

    @pl.when(jnp.logical_not(t_self))
    def _():
        t_copy().wait_recv()

    def slot(shift):
        return lax.rem(z + shift + chips, chips) * 2 + core

    def sc_piece(row):
        return strip_c.at[:, pl.ds(pl.multiple_of(row * 8, 8), 8), :]

    def ring_copy(a, way, s):
        sign = 1 - 2 * way
        row = slot(-sign * s)
        ref = sc_piece(row) if a == 0 else v_c.at[row]
        return pltpu.make_async_remote_copy(
            src_ref=ref, dst_ref=ref, send_sem=ring_s.at[a, way, s], recv_sem=ring_r.at[a, way, s],
            device_id=(slot(sign), c), device_id_type=MESH)

    def sib_copy(a, row):
        ref = sc_piece(row) if a == 0 else v_c.at[row]
        return pltpu.make_async_remote_copy(
            src_ref=ref, dst_ref=ref, send_sem=sib_s.at[a, row // 2], recv_sem=sib_r.at[a, row // 2],
            device_id=(2 * z + 1 - core, c), device_id_type=MESH)

    def ring_step(s):
        for a in range(2):
            ring_copy(a, 0, s).start()

            @pl.when(s < chips // 2 - 1)
            def _():
                ring_copy(a, 1, s).start()

            sib_copy(a, slot(-s)).start()

            @pl.when(s > 0)
            def _():
                sib_copy(a, slot(s)).start()

        for a in range(2):
            ring_copy(a, 0, s).wait_recv()

            @pl.when(s < chips // 2 - 1)
            def _():
                ring_copy(a, 1, s).wait_recv()

    loop(chips // 2, ring_step)
    for a in range(2):
        sib_copy(a, slot(chips // 2)).start()

    for copy in (sr_copy, d_copy, vp_copy, vr_copy):
        loop(cols - 1, lambda i: copy(i).wait_recv())
    for a in range(2):
        loop(chips, lambda i: sib_copy(a, 2 * i + core).wait_recv())
    loop(rows - 1, lambda i: z_copy(i).wait_send())
    partner_copy().wait_send()

    @pl.when(jnp.logical_not(t_self))
    def _():
        t_copy().wait_send()

    for copy in (sr_copy, d_copy, vp_copy, vr_copy):
        loop(cols - 1, lambda i: copy(i).wait_send())
    for a in range(2):
        loop(chips, lambda i: sib_copy(a, 2 * i + core).wait_send())
        loop(chips // 2, lambda s: ring_copy(a, 0, s).wait_send())
        loop(chips // 2 - 1, lambda s: ring_copy(a, 1, s).wait_send())


def gather(zin, srow, scol, child, pick, rows, cols):
    vmem = pl.BlockSpec(memory_space=pltpu.VMEM)
    dma = pltpu.SemaphoreType.DMA
    shape = jax.ShapeDtypeStruct
    width_r = srow.shape[2]
    width_c = scol.shape[2]
    return pl.pallas_call(
        comm_kernel,
        out_shape=(
            shape((3, PW, PW), F32),
            shape((2, PW, PW), BF16),
            shape((2, PW, width_r), F32),
            shape((2, PW, width_c), F32),
            shape((PW, width_r), BF16),
            shape((rows, 16, width_r), BF16),
        ),
        in_specs=[vmem] * 5,
        out_specs=(vmem,) * 6,
        scratch_shapes=[
            pltpu.VMEM((rows, 8, 128), F32),
            pltpu.VMEM((4, 16, TS), BF16),
            pltpu.VMEM((16, width_r), BF16),
            pltpu.VMEM((3, 16, PW), F32),
            pltpu.VMEM((2, 16, PW), BF16),
            dma((rows - 1,)), dma((rows - 1,)), dma, dma, dma, dma,
            dma((4, cols - 1)), dma((4, cols - 1)),
            dma((2, 2, rows // 4)), dma((2, 2, rows // 4)),
            dma((2, rows // 2)), dma((2, rows // 2)),
        ],
        compiler_params=pltpu.CompilerParams(
            collective_id=0, has_side_effects=True, vmem_limit_bytes=32 << 20),
    )(zin, srow, scol, child, pick)


def split3(x):
    high = x.astype(BF16)
    rest = x - high.astype(F32)
    mid = rest.astype(BF16)
    return high, mid, (rest - mid.astype(F32)).astype(BF16)


def dot6(a, b, ca, cb):
    ah, am, al = split3(a)
    bh, bm, bl = split3(b)
    left = jnp.concatenate([ah, ah, am, ah, al, am], axis=ca)
    right = jnp.concatenate([bh, bm, bh, bl, bh, bm], axis=cb)
    return lax.dot_general(left, right, (((ca,), (cb,)), ((), ())), preferred_element_type=F32)


def dot1(a, b, ca, cb):
    return lax.dot_general(a, b, (((ca,), (cb,)), ((), ())), preferred_element_type=F32)


def dot32(a, b):
    return lax.dot_general(
        a, b, (((1,), (0,)), ((), ())), precision=lax.Precision.HIGHEST, preferred_element_type=F32)


def block_inverse(block):
    ii = lax.broadcasted_iota(jnp.int32, (NB, 128), 0)
    ll = lax.broadcasted_iota(jnp.int32, (NB, 128), 1)
    m = jnp.where(ll < NB, block, jnp.where(ll == ii + NB, 1.0, 0.0).astype(F32))
    done = []
    for g in range(NB // SUB):
        low = SUB * g
        rows = [m[low + i : low + i + 1, :] for i in range(SUB)]
        s = {}
        for i in range(SUB):
            for k in range(i, SUB):
                s[i, k] = jnp.broadcast_to(rows[i][:, low + k : low + k + 1], (1, 128))
        for j in range(SUB):
            inv = lax.rsqrt(s[j, j])
            for k in range(j, SUB):
                s[j, k] = s[j, k] * inv
            rows[j] = rows[j] * inv
            for i in range(j + 1, SUB):
                for k in range(i, SUB):
                    s[i, k] = s[i, k] - s[j, i] * s[j, k]
                rows[i] = rows[i] - s[j, i] * rows[j]
        upper = jnp.concatenate(rows, axis=0)
        done.append(upper)
        if low + SUB < NB:
            across = jnp.transpose(jnp.concatenate([upper] * (128 // SUB), axis=0))
            for j in range(SUB):
                column = jnp.where(ii[:, 0:1] >= low + SUB, across[:NB, j : j + 1], 0.0)
                m = m - column * rows[j]
    return jnp.concatenate(done, axis=0)[:, NB : 2 * NB]


def factor(work):
    lane = lax.broadcasted_iota(jnp.int32, (NB, PW), 1)

    def step(b):
        here = pl.ds(pl.multiple_of(b * NB, NB), NB)
        band = work[here, :]
        lead = pltpu.roll(band[:, :PW], PW - b * NB, axis=1)
        inverse = block_inverse(lead[:, :128])
        upper = dot6(inverse, band, 1, 0)
        below = jnp.where(lane >= (b + 1) * NB, upper[:, :PW], 0.0)
        work[...] -= dot6(below, upper, 0, 0)
        work[here, :] = upper

    loop(PW // NB, step)


def panel_kernel(diag, vpiv, strip_r, strip_c, v_r, v_c, flags, out_a, out_b, work, wp, x0, x1, p01):
    i = lax.broadcasted_iota(jnp.int32, (PW, PW), 0)
    j = lax.broadcasted_iota(jnp.int32, (PW, PW), 1)
    eye = jnp.where(i == j, 1.0, 0.0).astype(F32)
    flag_p = flags[2:3, :PW].astype(BF16)
    for k in range(2):
        vp = vpiv[k]
        wp[k, PW:, :] = vp * flag_p
        wp[k, :PW, :] = vp - vp * flag_p
    work[:, :PW] = diag[0] + dot1(wp[0], wp[0], 0, 0)
    work[:, PW:] = eye
    factor(work)
    x0[...] = work[:, PW:]
    low = diag[1] + dot1(wp[1], wp[0], 0, 0)
    p01[...] = lax.dot_general(
        low, x0[...], (((1,), (1,)), ((), ())),
        precision=lax.Precision.HIGHEST, preferred_element_type=F32).astype(BF16)
    work[:, :PW] = diag[2] + dot1(wp[1], wp[1], 0, 0) - dot1(p01[...], p01[...], 1, 1)
    work[:, PW:] = eye
    factor(work)
    x1[...] = work[:, PW:]

    def tile(strip, v, flag, out, lanes, at, sign):
        flag = flag.astype(BF16)
        top = v - v * flag
        bottom = v * flag
        out[0:PW, at] = top
        out[PW : 2 * PW, at] = bottom
        w = jnp.concatenate([top, bottom], axis=0)
        s0 = strip[0, :, at] + dot1(wp[0], w, 0, 0)
        first = dot32(x0[...], s0).astype(BF16)
        out[2 * PW : 3 * PW, at] = first * sign
        s1 = strip[1, :, at] + dot1(wp[1], w, 0, 0) - dot1(p01[...], first, 1, 0)
        second = dot32(x1[...], s1).astype(BF16)
        out[3 * PW : 4 * PW, at] = second * sign

    rows_wide = v_r.shape[1]
    for h in range(rows_wide // PW):
        at = slice(h * PW, (h + 1) * PW)
        tile(strip_r, v_r[:, at], flags[1:2, at], out_a, PW, at, BF16(1))
    half = v_c.shape[0]
    for q in range(2):
        for h in range(rows_wide // PW):
            sub = slice(h * PW, (h + 1) * PW)
            at = slice(q * rows_wide + h * PW, q * rows_wide + (h + 1) * PW)
            v = v_c[:, q, :, sub].reshape(half * 16, PW)
            tile(strip_c, v, flags[0:1, at], out_b, PW, at, BF16(-1))


def panels(diag, vpiv, strip_r, strip_c, v_r, v_c, flags):
    vmem = pl.BlockSpec(memory_space=pltpu.VMEM)
    shape = jax.ShapeDtypeStruct
    v_c = v_c.reshape(v_c.shape[0] // 2, 2, 16, v_c.shape[2])
    return pl.pallas_call(
        panel_kernel,
        out_shape=(shape((4 * PW, strip_r.shape[2]), BF16), shape((4 * PW, strip_c.shape[2]), BF16)),
        in_specs=[vmem] * 7,
        out_specs=(vmem, vmem),
        scratch_shapes=[
            pltpu.VMEM((PW, 2 * PW), F32),
            pltpu.VMEM((2, 2 * PW, PW), BF16),
            pltpu.VMEM((PW, PW), F32),
            pltpu.VMEM((PW, PW), F32),
            pltpu.VMEM((PW, PW), BF16),
        ],
        compiler_params=pltpu.CompilerParams(vmem_limit_bytes=40 << 20),
    )(diag, vpiv, strip_r, strip_c, v_r, v_c, flags)


def final_kernel(front, left, right, scale, schur, panel):
    g = pl.program_id(0)
    r = lax.axis_index("row")
    c = lax.axis_index("col")
    rows, wide = schur.shape
    ii = lax.broadcasted_iota(jnp.int32, (rows, wide), 0)
    jj = lax.rem(lax.broadcasted_iota(jnp.int32, (rows, wide), 1) + g * wide, MT)
    keep = jnp.logical_and(ii >= 16, jj >= 16)
    total = front[...] * scale[0:1, :] + dot1(left[...], right[...], 0, 0)
    schur[...] = jnp.where(keep, total, 0.0)

    @pl.when(g == 0)
    def _():
        at = pl.multiple_of(c * 16, 16)
        m = lax.broadcasted_iota(jnp.int32, (16, rows), 0) + c * 16
        a = lax.broadcasted_iota(jnp.int32, (16, rows), 1)
        p0 = left[pl.ds(2 * PW + at, 16), :].astype(F32)
        p1 = left[pl.ds(3 * PW + at, 16), :].astype(F32)
        p0 = jnp.where(jnp.logical_or(a >= 8, m <= r * 8 + a), p0, 0.0)
        p1 = jnp.where(jnp.logical_or(a >= 16, m <= r * 8 + a - 8), p1, 0.0)
        p1 = jnp.where(a >= 8, p1, 0.0)
        panel[...] = jnp.transpose(jnp.concatenate([p0, p1], axis=0)).astype(BF16)


def final(front, left, right, scale):
    rows, wide = front.shape
    step = 256
    return pl.pallas_call(
        final_kernel,
        grid=(wide // step,),
        out_shape=(
            jax.ShapeDtypeStruct((rows, wide), F32),
            jax.ShapeDtypeStruct((rows, 32), BF16),
        ),
        in_specs=[
            pl.BlockSpec((rows, step), lambda g: (0, g)),
            pl.BlockSpec((4 * PW, rows), lambda g: (0, 0)),
            pl.BlockSpec((4 * PW, step), lambda g: (0, g)),
            pl.BlockSpec((8, step), lambda g: (0, g)),
        ],
        out_specs=(
            pl.BlockSpec((rows, step), lambda g: (0, g)),
            pl.BlockSpec((rows, 32), lambda g: (0, 0)),
        ),
        compiler_params=pltpu.CompilerParams(vmem_limit_bytes=32 << 20),
    )(front, left, right, scale)


def local(front, tile_group, child, row_map):
    rows = lax.axis_size("row")
    cols = lax.axis_size("col")
    r = lax.axis_index("row")
    c = lax.axis_index("col")
    height, width = front.shape
    tiles = height // TS
    group_r = lax.dynamic_slice_in_dim(tile_group, r, 1)
    group_c = lax.dynamic_slice_in_dim(tile_group, 2 * c, 2)
    same = (group_r == group_c).astype(F32)
    scale = jnp.broadcast_to(jnp.repeat(same, MT)[None, :], (8, width))

    wide = front.reshape(height, 2, MT)[:, :, :16].reshape(height, 2, 2, 8) * same[None, :, None, None]
    srow = wide.transpose(2, 1, 3, 0).reshape(2, 16, height)
    scol = (front[:16] * scale[0:1]).reshape(2, 8, width)

    own_map = lax.dynamic_slice_in_dim(row_map, r * tiles, tiles)
    other = jnp.bitwise_xor(r, rows // 2)
    partner_map = lax.dynamic_slice_in_dim(row_map, other * tiles, tiles)
    both = jnp.concatenate([own_map, partner_map])
    pick = (both[None, :] == (r * tiles + jnp.arange(tiles, dtype=jnp.int32))[:, None]).astype(F32)
    pick = jnp.broadcast_to(pick.reshape(8 * tiles, 1), (8 * tiles, TS))

    corner = wide[:16].reshape(2, 8, 2, 2, 8)
    heads = child.reshape(tiles, TS, 16)[:, :16].astype(F32)
    parts = []
    for target in (r, other):
        chosen = (own_map == target * tiles).astype(F32)
        parts.append(jnp.sum(heads * chosen[:, None, None], axis=0).reshape(2, 8, 16))
    zin = jnp.concatenate(
        [
            corner[0, :, :, 0, :].reshape(8, 16),
            corner[0, :, :, 1, :].reshape(8, 16),
            corner[1, :, :, 1, :].reshape(8, 16),
            jnp.zeros((8, 16), F32),
            parts[0][0], parts[1][0], parts[0][1], parts[1][1],
        ],
        axis=1,
    )

    count = row_map.shape[0]
    second = (row_map[count // 2 :, None] == jnp.arange(count, dtype=jnp.int32)[None, :]).any(axis=0)
    second = second.astype(F32)
    flag_c = jnp.repeat(lax.dynamic_slice_in_dim(second, 2 * c * tiles, 2 * tiles), TS)
    flag_r = jnp.repeat(lax.dynamic_slice_in_dim(second, r * tiles, tiles), TS)
    flag_p = jnp.repeat(second[::tiles], 8)
    flags = jnp.stack([
        flag_c,
        jnp.concatenate([flag_r, jnp.zeros((width - height,), F32)]),
        jnp.concatenate([flag_p, jnp.zeros((width - PW,), F32)]),
    ])
    flags = jnp.concatenate([flags, jnp.zeros((5, width), F32)])

    child_t = child.reshape(tiles, TS, 16).transpose(0, 2, 1)
    gathered = gather(zin, srow, scol, child_t, pick, rows, cols)
    left, right = panels(*gathered, flags)
    schur, panel = final(front, left, right, scale)
    return panel, schur


def solution(mesh):
    placed = (P("row", "col"), P(), P("row", "col"), P())
    return jax.shard_map(
        local,
        mesh=mesh,
        in_specs=placed,
        out_specs=(P("row", "col"), P("row", "col")),
        check_vma=False,
    )
```

time: 1310 us -> 134 us (0.10)
  the two profiles are of different devices: /device:TPU:6 before, /device:TPU:5 now
where the time goes in v1:
time: 134 us; the launch traced here: 133 us
  Pallas kernels  112 us (84%)
  local copies, waits for them, and re-layouts  15.9 us (12%)
  other arithmetic  4.41 us (3%)
    pallas_call x1, Pallas kernels, gather(): pl.pallas_call(comm_kernel, out_shape=(shape((3, PW, PW), F32), shape((2,...  76.7 us
    pallas_call x1, Pallas kernels, panels(): pl.pallas_call(panel_kernel, out_shape=(shape((4 * PW, strip_r.shape[2]),...  32.1 us
    unnamed x30, local copies, waits for them, and re-layouts  12.5 us
    pallas_call x1, Pallas kernels, final(): pl.pallas_call(final_kernel, grid=(wide // step,), out_shape=(jax.ShapeDt...  3.51 us

profile of v1, /device:TPU:5, one launch (start us, length us, event | category | flops | bytes accessed | tf_op | source)
XLA Modules:
  0.0 133.4 jit_solution(12649762087776897325)
XLA Ops:
  0.6 0.7 compare_convert_fusion.2
  1.4 0.7 reshape.75
  2.1 0.1 fusion.2
  2.2 0.1 fusion.5
  2.3 0.1 copy.39
  2.4 0.1 copy.40
  2.4 0.1 copy.41
  2.5 0.1 copy.42
  2.6 1.2 dynamic_slice.18
  3.8 1.4 %compare_convert_fusion.3 = f32[2]{0:T(128)S(1)} fusion(s32[32]{0:T(128)} %param.5, s32[]{:T(128)S(6)} %select_n.17, s32[]{:T(128)} %bitcast.2), kind=kLoop, calls=%fused_computation.16 | loop fusion | flops 4 | bytes 24 | tf_op jit(solution)/shard_map/convert_element_type | solution.py:441
  5.2 3.0 %copy.25 = f32[512,1024]{0,1:T(8,128)} copy(f32[512,1024]{1,0:T(8,128)} %front.1) | data formatting | bytes 4194304 | tf_op args[0]
  8.2 0.9 fusion
  9.1 0.1 reshape.74
  9.3 0.1 copy.36
  9.3 0.1 copy.37
  9.4 0.1 copy.38
  9.5 0.1 concatenate.15.zin
  9.6 0.1 dynamic_slice.21
  9.6 0.1 pad_add_fusion
  9.7 0.1 compare_convert_fusion
  9.8 0.1 reshape.81
  9.9 0.1 broadcast_in_dim.42.pick
  9.9 0.9 copy_bitcast_fusion.srow
  10.9 0.1 broadcast_bitcast_fusion
  11.0 76.7 %shard_map.59 = (f32[3,256,256]{2,1,0:T(8,128)S(1)}, bf16[2,256,256]{2,1,0:T(8,128)(2,1)S(1)}, f32[2,256,512]{2,1,0:T(8,128)S(1)}, f32[2,256,1024]{2,1,0:T(8,128...) custom-call(f32[8,128]{1,0:T(8,128)S(1)} %concatenate.15.zin, ...), custom_call_target="tpu_custom_call" | custom-call | tf_op jit(solution)/shard_map/pallas_call | solution.py:216
  87.7 0.0 copy-start.1
  87.7 1.3 copy-done.1
  89.0 0.9 copy-done.3
  89.9 0.8 copy-done.5
  90.7 0.7 copy-done.7
  91.4 0.1 slice.55
  91.4 0.1 fusion.3
  91.5 0.1 dynamic_slice.23
  91.6 0.1 broadcast_bitcast_fusion.1
  91.7 0.1 dynamic_slice.22
  91.8 0.1 broadcast_in_dim.43
  91.9 0.1 slice.56
  92.0 0.1 broadcast_in_dim.45
  92.0 0.1 reshape.80
  92.2 0.1 pad.5.clone
  92.2 0.1 maximum_maximum_fusion.flags
  92.3 1.6 %copy-done.2 = f32[2,256,1024]{2,1,0:T(8,128)S(1)} copy-done((f32[2,256,1024]{2,1,0:T(8,128)S(1)}, f32[2,256,1024]{2,1,0:T(8,128)}, u32[]{:S(2)}) %copy-start.2) | copy-done | bytes 2097176
  93.9 1.1 copy-done.4
  95.0 1.0 copy-done.6
  96.1 0.9 copy-done.8
  97.0 32.1 %shard_map.60 = (bf16[1024,512]{1,0:T(8,128)(2,1)S(1)}, bf16[1024,1024]{1,0:T(8,128)(2,1)S(1)}) custom-call(f32[3,256,256]{2,1,0:T(8,128)S(1)} %copy-done.4, bf16[2,256,256]{2,1,0:T(8,128)(2,1)S(1)} %get-tuple-element.13.vpiv, f32[2,256,512]{2,1,0:T(8,128)S(1)} %get-tuple-element.14.strip_r, f32[2,256,1024]{2,1,0:T(8,128)S(1)} %copy-done.2, ...), custom_call_target="tpu_custom_call" | custom-call | tf_op jit(solution)/shard_map/pallas_call | solution.py:368
  129.2 3.5 %shard_map.61 = (f32[512,1024]{1,0:T(8,128)}, bf16[512,32]{1,0:T(8,128)(2,1)S(1)}) custom-call(f32[512,1024]{1,0:T(8,128)S(1)} %copy-done, bf16[1024,512]{1,0:T(8,128)(2,1)S(1)} %get-tuple-element.18.left, bf16[1024,1024]{1,0:T(8,128)(2,1)S(1)} %get-tuple-element.19.right, f32[8,1024]{1,0:T(8,128)S(1)} %broadcast_in_dim.47.scale), custom_call_target="tpu_custom_call" | custom-call | tf_op jit(solution)/shard_map/pallas_call | solution.py:411
  132.7 0.7 copy.35
  (26 shorter events, 0.1 us)
Async XLA Ops:
  5.2 4.4 %copy-start.10 = (s32[128]{0:T(128)S(1)}, s32[128]{0:T(128)}, u32[]{:S(2)}) copy-start(s32[128]{0:T(128)} %param.7) | copy-start | bytes 1540
  5.2 5.8 %copy-start = (f32[512,1024]{1,0:T(8,128)S(1)}, f32[512,1024]{1,0:T(8,128)}, u32[]{:S(2)}) copy-start(f32[512,1024]{1,0:T(8,128)} %front.1) | copy-start | bytes 6291460
  5.2 5.8 %copy-start.9 = (bf16[512,16]{0,1:T(8,128)(2,1)S(1)}, bf16[512,16]{0,1:T(8,128)(2,1)}, u32[]{:S(2)}) copy-start(bf16[512,16]{0,1:T(8,128)(2,1)} %param.6) | copy-start | bytes 49156
  87.7 1.3 copy-start.1
  89.0 0.9 copy-start.3
  89.9 0.8 copy-start.5
  90.7 0.7 copy-start.7
  92.3 1.6 %copy-start.2 = (f32[2,256,1024]{2,1,0:T(8,128)S(1)}, f32[2,256,1024]{2,1,0:T(8,128)}, u32[]{:S(2)}) copy-start(f32[2,256,1024]{2,1,0:T(8,128)} %copy-done.1) | copy-start | bytes 6291460
  93.9 1.1 copy-start.4
  95.0 1.0 copy-start.6
  96.1 0.9 copy-start.8

commit v2 on v0

v2 whole, which is shorter than its diff:
```python
import functools

import jax
import jax.numpy as jnp
from jax import lax
from jax.experimental import pallas as pl
from jax.experimental.pallas import tpu as pltpu
from jax.sharding import PartitionSpec as P

PW = 256
NP = 2
TS = 128
MT = 512
NB = 32
SUB = 8
F32 = jnp.float32
BF16 = jnp.bfloat16
MESH = pl.DeviceIdType.MESH


def loop(count, body):
    def step(i, carry):
        body(i)
        return carry

    lax.fori_loop(0, count, step, 0)


def split3(x):
    high = x.astype(BF16)
    rest = x - high.astype(F32)
    mid = rest.astype(BF16)
    return high, mid, (rest - mid.astype(F32)).astype(BF16)


def dot6(a, b, ca, cb):
    ah, am, al = split3(a)
    bh, bm, bl = split3(b)
    left = jnp.concatenate([ah, ah, am, ah, al, am], axis=ca)
    right = jnp.concatenate([bh, bm, bh, bl, bh, bm], axis=cb)
    return lax.dot_general(left, right, (((ca,), (cb,)), ((), ())), preferred_element_type=F32)


def dot1(a, b, ca, cb):
    return lax.dot_general(a, b, (((ca,), (cb,)), ((), ())), preferred_element_type=F32)


def block_inverse(block):
    ii = lax.broadcasted_iota(jnp.int32, (NB, 128), 0)
    ll = lax.broadcasted_iota(jnp.int32, (NB, 128), 1)
    m = jnp.where(ll < NB, block, jnp.where(ll == ii + NB, 1.0, 0.0).astype(F32))
    done = []
    for g in range(NB // SUB):
        low = SUB * g
        rows = [m[low + i : low + i + 1, :] for i in range(SUB)]
        s = {}
        for i in range(SUB):
            for k in range(i, SUB):
                s[i, k] = jnp.broadcast_to(rows[i][:, low + k : low + k + 1], (1, 128))
        for j in range(SUB):
            inv = lax.rsqrt(s[j, j])
            for k in range(j, SUB):
                s[j, k] = s[j, k] * inv
            rows[j] = rows[j] * inv
            for i in range(j + 1, SUB):
                for k in range(i, SUB):
                    s[i, k] = s[i, k] - s[j, i] * s[j, k]
                rows[i] = rows[i] - s[j, i] * rows[j]
        upper = jnp.concatenate(rows, axis=0)
        done.append(upper)
        if low + SUB < NB:
            across = jnp.transpose(jnp.concatenate([upper] * (128 // SUB), axis=0))
            for j in range(SUB):
                column = jnp.where(ii[:, 0:1] >= low + SUB, across[:NB, j : j + 1], 0.0)
                m = m - column * rows[j]
    return jnp.concatenate(done, axis=0)[:, NB : 2 * NB]


def factor(work, beside):
    lane = lax.broadcasted_iota(jnp.int32, (NB, PW), 1)

    def step(b):
        beside(b)
        here = pl.ds(pl.multiple_of(b * NB, NB), NB)
        band = work[here, :]
        lead = pltpu.roll(band[:, :PW], PW - b * NB, axis=1)
        inverse = block_inverse(lead[:, :128])
        upper = dot6(inverse, band, 1, 0)
        below = jnp.where(lane >= (b + 1) * NB, upper[:, :PW], 0.0)
        work[...] -= dot6(below, upper, 0, 0)
        work[here, :] = upper

    loop(PW // NB, step)


def split2(x, axis):
    high = x.astype(BF16)
    low = (x - high.astype(F32)).astype(BF16)
    return high, low


def left3(x):
    high, low = split2(x, 1)
    return jnp.concatenate([high, high, low], axis=1)


def right3(x, axis):
    high, low = split2(x, axis)
    return jnp.concatenate([high, low, high], axis=axis)


def front_kernel(
    front, child, groups, tile_map, map_lanes,
    out_a, out_b,
    zin, srow, zbuf, partner, placed, dpiece, vpiece,
    diag, vpiv, strip_r, strip_c, v_r, v_c, flags,
    work, wp, x0, x1, p01,
    z_s, z_r, p_s, p_r, t_s, t_r,
    plane_s, plane_r, ring_s, ring_r, sib_s, sib_r,
):
    r = lax.axis_index("row")
    c = lax.axis_index("col")
    rows = lax.axis_size("row")
    cols = lax.axis_size("col")
    height, width = front.shape
    z = r // 2
    core = r % 2
    chips = rows // 2
    other = lax.rem(r + chips, rows)
    t_row = 2 * c + core
    t_col = z
    t_self = jnp.logical_and(t_row == r, t_col == c)

    barrier = pltpu.get_barrier_semaphore()

    def hello_row(i):
        pl.semaphore_signal(barrier, inc=1, device_id=(lax.rem(r + i + 1, rows), c), device_id_type=MESH)

    def hello_col(i):
        pl.semaphore_signal(barrier, inc=1, device_id=(r, lax.rem(c + i + 1, cols)), device_id_type=MESH)

    loop(rows - 1, hello_row)
    loop(cols - 1, hello_col)

    @pl.when(jnp.logical_not(t_self))
    def _():
        pl.semaphore_signal(barrier, inc=1, device_id=(t_row, t_col), device_id_type=MESH)

    def one_if(same):
        return jnp.where(same, 1.0, 0.0).astype(F32)

    coupled = [one_if(groups[r] == groups[2 * c + q]) for q in range(2)]
    turned = []
    for q in range(2):
        t = jnp.transpose(front[:, q * MT : q * MT + 128])[:16] * coupled[q]
        srow[0, 8 * q : 8 * q + 8, :] = t[:8]
        srow[1, 8 * q : 8 * q + 8, :] = t[8:]
        turned.append(t[:, :128])
    own_maps = [tile_map[4 * r + t] for t in range(4)]
    other_maps = [tile_map[4 * other + t] for t in range(4)]
    heads = []
    for target in (r, other):
        total = jnp.zeros((16, TS), F32)
        for t in range(4):
            total = total + child[:, t * TS : (t + 1) * TS].astype(F32) * one_if(own_maps[t] == 4 * target)
        heads.append(total)

    def second8(x):
        return pltpu.roll(x, 120, axis=1)

    tall = jnp.concatenate(
        [
            turned[0][:8], turned[1][:8], turned[0][8:], turned[1][8:],
            second8(turned[0])[8:], second8(turned[1])[8:], jnp.zeros((16, 128), F32),
            heads[0], heads[1], second8(heads[0]), second8(heads[1]),
        ],
        axis=0,
    )
    zin[...] = jnp.transpose(tall)[:8]

    pl.semaphore_wait(barrier, rows + cols - 2 + jnp.where(t_self, 0, 1))

    def z_copy(i):
        return pltpu.make_async_remote_copy(
            src_ref=zin, dst_ref=zbuf.at[r], send_sem=z_s.at[i], recv_sem=z_r.at[i],
            device_id=(lax.rem(r + i + 1, rows), c), device_id_type=MESH)

    def partner_copy():
        return pltpu.make_async_remote_copy(
            src_ref=child, dst_ref=partner, send_sem=p_s, recv_sem=p_r,
            device_id=(other, c), device_id_type=MESH)

    loop(rows - 1, lambda i: z_copy(i).start())
    partner_copy().start()
    zbuf[pl.ds(r, 1)] = zin[...][None]

    own8 = pl.ds(pl.multiple_of(r * 8, 8), 8)
    own16 = pl.ds(pl.multiple_of(c * 16, 16), 16)
    for k in range(2):
        for q in range(2):
            strip_c[k, own8, q * MT : (q + 1) * MT] = (
                front[8 * k : 8 * k + 8, q * MT : (q + 1) * MT] * coupled[q])
    strip_r[:, own16, :] = srow[...]

    listed = jnp.transpose(jnp.broadcast_to(map_lanes[...].astype(F32), (128, 128)))
    count = map_lanes.shape[1]
    at_lane = lax.broadcasted_iota(jnp.int32, (128, 128), 1).astype(F32)
    child_id = lax.broadcasted_iota(jnp.int32, (128, 128), 0)
    hits = jnp.where(jnp.logical_and(listed == at_lane, child_id >= count // 2), 1.0, 0.0)
    second = jnp.broadcast_to(jnp.sum(hits, axis=0, keepdims=True), (8, 128)).astype(BF16)

    def spread(tile_of_lane, lanes):
        tile = lax.broadcasted_iota(jnp.int32, (128, lanes), 0)
        lane = lax.broadcasted_iota(jnp.int32, (128, lanes), 1)
        chosen = jnp.where(tile == tile_of_lane(lane), 1.0, 0.0).astype(BF16)
        return dot1(second, chosen, 1, 0).astype(BF16)

    flag_p = spread(lambda lane: 4 * lax.shift_right_logical(lane, 3), PW)[0:1]
    flags[0:8, :height] = spread(lambda lane: 4 * r + lax.shift_right_logical(lane, 7), height).astype(F32)
    flags[0:8, height:] = spread(lambda lane: 8 * c + lax.shift_right_logical(lane, 7), width).astype(F32)

    def plane_copy(a, src, dst, i):
        return pltpu.make_async_remote_copy(
            src_ref=src, dst_ref=dst, send_sem=plane_s.at[a, i], recv_sem=plane_r.at[a, i],
            device_id=(r, lax.rem(c + i + 1, cols)), device_id_type=MESH)

    def sr_copy(i):
        return plane_copy(0, srow, strip_r.at[:, own16, :], i)

    def d_copy(i):
        return plane_copy(1, dpiece.at[0], diag.at[0, own16, :], i)

    def d1_copy(i):
        return plane_copy(4, dpiece.at[pl.ds(1, 2)], diag.at[pl.ds(1, 2), own16, :], i)

    def vp_copy(i):
        return plane_copy(2, vpiece, vpiv.at[:, own16, :], i)

    def vr_copy(i):
        return plane_copy(3, placed, v_r.at[own16, :], i)

    loop(rows - 1, lambda i: z_copy(i).wait_recv())
    flat = jnp.transpose(zbuf[...].reshape(rows * 8, 128))
    dpiece[0] = flat[0:16]
    dpiece[1] = flat[16:32]
    dpiece[2] = flat[32:48]
    half = rows * 4

    def swapped_halves(x):
        return jnp.concatenate([x[:, half:], x[:, :half]], axis=1)

    vpiece[0] = (flat[64:80] + swapped_halves(flat[80:96])).astype(BF16)
    vpiece[1] = (flat[96:112] + swapped_halves(flat[112:128])).astype(BF16)
    diag[:, own16, :] = dpiece[...]
    vpiv[:, own16, :] = vpiece[...]
    loop(cols - 1, lambda i: vp_copy(i).start())
    loop(cols - 1, lambda i: d_copy(i).start())
    loop(cols - 1, lambda i: d1_copy(i).start())

    partner_copy().wait_recv()
    for j in range(height // TS):
        total = jnp.zeros((16, TS), F32)
        for t in range(4):
            at = slice(t * TS, (t + 1) * TS)
            total = total + child[:, at].astype(F32) * one_if(own_maps[t] == 4 * r + j)
            total = total + partner[:, at].astype(F32) * one_if(other_maps[t] == 4 * r + j)
        placed[:, j * TS : (j + 1) * TS] = total.astype(BF16)
    v_r[own16, :] = placed[...]

    def t_copy():
        return pltpu.make_async_remote_copy(
            src_ref=placed, dst_ref=v_c.at[t_row], send_sem=t_s, recv_sem=t_r,
            device_id=(t_row, t_col), device_id_type=MESH)

    @pl.when(t_self)
    def _():
        v_c[pl.ds(r, 1)] = placed[...][None]

    @pl.when(jnp.logical_not(t_self))
    def _():
        t_copy().start()

    loop(cols - 1, lambda i: vr_copy(i).start())
    loop(cols - 1, lambda i: sr_copy(i).start())

    @pl.when(jnp.logical_not(t_self))
    def _():
        t_copy().wait_recv()

    def slot(shift):
        return lax.rem(z + shift + chips, chips) * 2 + core

    def piece(a, row):
        if a == 0:
            return strip_c.at[:, pl.ds(pl.multiple_of(row * 8, 8), 8), :]
        return v_c.at[row]

    def ring_copy(a, way, s):
        sign = 1 - 2 * way
        ref = piece(a, slot(-sign * s))
        return pltpu.make_async_remote_copy(
            src_ref=ref, dst_ref=ref, send_sem=ring_s.at[a, way, s], recv_sem=ring_r.at[a, way, s],
            device_id=(slot(sign), c), device_id_type=MESH)

    def sib_copy(a, row):
        ref = piece(a, row)
        return pltpu.make_async_remote_copy(
            src_ref=ref, dst_ref=ref, send_sem=sib_s.at[a, row // 2], recv_sem=sib_r.at[a, row // 2],
            device_id=(2 * z + 1 - core, c), device_id_type=MESH)

    hops = chips // 2

    def ring_start(s):
        for a in range(2):
            ring_copy(a, 0, s).start()

            @pl.when(s < hops - 1)
            def _():
                ring_copy(a, 1, s).start()

            sib_copy(a, slot(-s)).start()

            @pl.when(s > 0)
            def _():
                sib_copy(a, slot(s)).start()

    def ring_wait(s):
        for a in range(2):
            ring_copy(a, 0, s).wait_recv()

            @pl.when(s < hops - 1)
            def _():
                ring_copy(a, 1, s).wait_recv()

    ring_start(0)

    def ring_beside(first):
        def beside(b):
            s = first + b // 2

            @pl.when(b % 2 == 1)
            def _():
                ring_wait(s)

                @pl.when(s < hops - 1)
                def _():
                    ring_start(s + 1)

        return beside

    loop(cols - 1, lambda i: vp_copy(i).wait_recv())
    for k in range(2):
        vp = vpiv[k]
        wp[k, PW:, :] = vp * flag_p
        wp[k, :PW, :] = vp - vp * flag_p
    i = lax.broadcasted_iota(jnp.int32, (PW, PW), 0)
    j = lax.broadcasted_iota(jnp.int32, (PW, PW), 1)
    eye = jnp.where(i == j, 1.0, 0.0).astype(F32)
    outer = dot1(wp[0], wp[0], 0, 0)
    loop(cols - 1, lambda i: d_copy(i).wait_recv())
    work[:, :PW] = diag[0] + outer
    work[:, PW:] = eye
    factor(work, ring_beside(0))
    x0[...] = left3(work[:, PW:])
    loop(cols - 1, lambda i: d1_copy(i).wait_recv())
    low = diag[1] + dot1(wp[1], wp[0], 0, 0)
    p01[...] = dot1(right3(low, 1), x0[...], 1, 1).astype(BF16)

    work[:, :PW] = diag[2] + dot1(wp[1], wp[1], 0, 0) - dot1(p01[...], p01[...], 1, 1)
    work[:, PW:] = eye
    factor(work, ring_beside(hops // 2))
    x1[...] = left3(work[:, PW:])
    for a in range(2):
        sib_copy(a, slot(hops)).start()

    for copy in (sr_copy, vr_copy):
        loop(cols - 1, lambda i: copy(i).wait_recv())

    def tile(strip, v, flag, out, at, sign):
        flag = flag.astype(BF16)
        bottom = v * flag
        top = v - bottom
        out[0:PW, at] = top
        out[PW : 2 * PW, at] = bottom
        w = jnp.concatenate([top, bottom], axis=0)
        s0 = strip[0, :, at] + dot1(wp[0], w, 0, 0)
        first = dot1(x0[...], right3(s0, 0), 1, 0).astype(BF16)
        out[2 * PW : 3 * PW, at] = first * sign
        s1 = strip[1, :, at] + dot1(wp[1], w, 0, 0) - dot1(p01[...], first, 1, 0)
        second = dot1(x1[...], right3(s1, 0), 1, 0).astype(BF16)
        out[3 * PW : 4 * PW, at] = second * sign

    for h in range(height // PW):
        at = slice(h * PW, (h + 1) * PW)
        tile(strip_r, v_r[:, at], flags[0:1, at], out_a, at, BF16(1))
    for a in range(2):
        loop(chips, lambda i: sib_copy(a, 2 * i + core).wait_recv())
    for q in range(2):
        for h in range(height // PW):
            sub = slice(h * PW, (h + 1) * PW)
            at = slice(q * height + h * PW, q * height + (h + 1) * PW)
            v = jnp.concatenate([v_c[2 * i + q, :, sub] for i in range(chips)], axis=0)
            lanes = slice(height + at.start, height + at.stop)
            tile(strip_c, v, flags[0:1, lanes], out_b, at, BF16(-1))

    loop(rows - 1, lambda i: z_copy(i).wait_send())
    partner_copy().wait_send()

    @pl.when(jnp.logical_not(t_self))
    def _():
        t_copy().wait_send()

    for copy in (sr_copy, d_copy, d1_copy, vp_copy, vr_copy):
        loop(cols - 1, lambda i: copy(i).wait_send())
    for a in range(2):
        loop(chips, lambda i: sib_copy(a, 2 * i + core).wait_send())
        loop(hops, lambda s: ring_copy(a, 0, s).wait_send())
        loop(hops - 1, lambda s: ring_copy(a, 1, s).wait_send())


def panels(front, child, tile_group, row_map, rows, cols):
    vmem = pl.BlockSpec(memory_space=pltpu.VMEM)
    smem = pl.BlockSpec(memory_space=pltpu.SMEM)
    dma = pltpu.SemaphoreType.DMA
    shape = jax.ShapeDtypeStruct
    height, width = front.shape
    return pl.pallas_call(
        front_kernel,
        out_shape=(shape((4 * PW, height), BF16), shape((4 * PW, width), BF16)),
        in_specs=[vmem, vmem, smem, smem, vmem],
        out_specs=(vmem, vmem),
        scratch_shapes=[
            pltpu.VMEM((8, 128), F32),
            pltpu.VMEM((2, 16, height), F32),
            pltpu.VMEM((rows, 8, 128), F32),
            pltpu.VMEM((16, height), BF16),
            pltpu.VMEM((16, height), BF16),
            pltpu.VMEM((3, 16, PW), F32),
            pltpu.VMEM((2, 16, PW), BF16),
            pltpu.VMEM((3, PW, PW), F32),
            pltpu.VMEM((2, PW, PW), BF16),
            pltpu.VMEM((2, PW, height), F32),
            pltpu.VMEM((2, PW, width), F32),
            pltpu.VMEM((PW, height), BF16),
            pltpu.VMEM((rows, 16, height), BF16),
            pltpu.VMEM((8, height + width), F32),
            pltpu.VMEM((PW, 2 * PW), F32),
            pltpu.VMEM((2, 2 * PW, PW), BF16),
            pltpu.VMEM((PW, 3 * PW), BF16),
            pltpu.VMEM((PW, 3 * PW), BF16),
            pltpu.VMEM((PW, PW), BF16),
            dma((rows - 1,)), dma((rows - 1,)), dma, dma, dma, dma,
            dma((5, cols - 1)), dma((5, cols - 1)),
            dma((2, 2, rows // 4)), dma((2, 2, rows // 4)),
            dma((2, rows // 2)), dma((2, rows // 2)),
        ],
        compiler_params=pltpu.CompilerParams(
            collective_id=0, has_side_effects=True, vmem_limit_bytes=40 << 20),
    )(front, child, tile_group, row_map, row_map.reshape(1, -1))


def final_kernel(front, left, right, groups, schur, panel):
    g = pl.program_id(0)
    r = lax.axis_index("row")
    c = lax.axis_index("col")
    rows, wide = schur.shape
    ii = lax.broadcasted_iota(jnp.int32, (rows, wide), 0)
    jj = lax.rem(lax.broadcasted_iota(jnp.int32, (rows, wide), 1) + g * wide, MT)
    keep = jnp.logical_and(ii >= 16, jj >= 16)
    coupled = jnp.where(groups[r] == groups[2 * c + (g * wide) // MT], 1.0, 0.0).astype(F32)
    total = front[...] * coupled + dot1(left[...], right[...], 0, 0)
    schur[...] = jnp.where(keep, total, 0.0)

    @pl.when(g == 0)
    def _():
        at = pl.multiple_of(c * 16, 16)
        m = lax.broadcasted_iota(jnp.int32, (16, rows), 0) + c * 16
        a = lax.broadcasted_iota(jnp.int32, (16, rows), 1)
        p0 = left[pl.ds(2 * PW + at, 16), :].astype(F32)
        p1 = left[pl.ds(3 * PW + at, 16), :].astype(F32)
        p0 = jnp.where(jnp.logical_or(a >= 8, m <= r * 8 + a), p0, 0.0)
        p1 = jnp.where(jnp.logical_or(a >= 16, m <= r * 8 + a - 8), p1, 0.0)
        p1 = jnp.where(a >= 8, p1, 0.0)
        panel[0:16, :] = p0.astype(BF16)
        panel[16:32, :] = p1.astype(BF16)


def final(front, left, right, tile_group):
    rows, wide = front.shape
    step = 256
    return pl.pallas_call(
        final_kernel,
        grid=(wide // step,),
        out_shape=(
            jax.ShapeDtypeStruct((rows, wide), F32),
            jax.ShapeDtypeStruct((32, rows), BF16),
        ),
        in_specs=[
            pl.BlockSpec((rows, step), lambda g: (0, g)),
            pl.BlockSpec((4 * PW, rows), lambda g: (0, 0)),
            pl.BlockSpec((4 * PW, step), lambda g: (0, g)),
            pl.BlockSpec(memory_space=pltpu.SMEM),
        ],
        out_specs=(
            pl.BlockSpec((rows, step), lambda g: (0, g)),
            pl.BlockSpec((32, rows), lambda g: (0, 0)),
        ),
        compiler_params=pltpu.CompilerParams(vmem_limit_bytes=32 << 20),
    )(front, left, right, tile_group)


def local(front, tile_group, child, row_map):
    rows = lax.axis_size("row")
    cols = lax.axis_size("col")
    left, right = panels(front, child.T, tile_group, row_map, rows, cols)
    schur, panel = final(front, left, right, tile_group)
    return panel.T, schur


def solution(mesh):
    placed = (P("row", "col"), P(), P("row", "col"), P())
    return jax.shard_map(
        local,
        mesh=mesh,
        in_specs=placed,
        out_specs=(P("row", "col"), P("row", "col")),
        check_vma=False,
    )
```

time: 1310 us -> 92.3 us (0.07)
  the two profiles are of different devices: /device:TPU:6 before, /device:TPU:4 now
where the time goes in v2:
time: 92.3 us; the launch traced here: 92.1 us
  Pallas kernels  87.8 us (95%)
  local copies, waits for them, and re-layouts  3.61 us (4%)
    pallas_call x1, Pallas kernels, panels(): pl.pallas_call(front_kernel, out_shape=(shape((4 * PW, height), BF16), sh...  83.9 us
    pallas_call x1, Pallas kernels, final(): pl.pallas_call(final_kernel, grid=(wide // step,), out_shape=(jax.ShapeDt...  3.87 us
    unnamed x8, local copies, waits for them, and re-layouts  3.61 us

profile of v2, /device:TPU:4, one launch (start us, length us, event | category | flops | bytes accessed | tf_op | source)
XLA Modules:
  0.0 92.1 jit_solution(17475254767587648367)
XLA Ops:
  0.6 0.0 copy-start
  0.6 1.6 %copy-done = f32[512,1024]{1,0:T(8,128)S(1)} copy-done((f32[512,1024]{1,0:T(8,128)S(1)}, f32[512,1024]{1,0:T(8,128)}, u32[]{:S(2)}) %copy-start) | copy-done | bytes 2097176
  2.2 0.0 copy-start.1
  2.2 0.7 copy-done.1
  2.9 0.0 copy-start.2
  2.9 0.7 copy-done.2
  3.6 0.0 copy-start.3
  3.6 0.7 copy-done.3
  4.3 83.9 %shard_map.59 = (bf16[1024,512]{1,0:T(8,128)(2,1)S(1)}, bf16[1024,1024]{1,0:T(8,128)(2,1)S(1)}) custom-call(f32[512,1024]{1,0:T(8,128)S(1)} %copy-done, bf16[16,512]{1,0:T(8,128)(2,1)S(1)} %bitcast.3, s32[32]{0:T(128)S(1)} %copy-done.3, s32[128]{0:T(128)S(1)} %copy-done.2, s32[1,128]{1,0:T(1,128)S(1)} %bitcast.4), custom_call_target="tpu_custom_call" | custom-call | tf_op jit(solution)/shard_map/pallas_call | solution.py:427
  88.2 3.9 %shard_map.60 = (f32[512,1024]{1,0:T(8,128)}, bf16[32,512]{1,0:T(8,128)(2,1)}) custom-call(f32[512,1024]{1,0:T(8,128)S(1)} %copy-done, bf16[1024,512]{1,0:T(8,128)(2,1)S(1)} %get-tuple-element.6.left, bf16[1024,1024]{1,0:T(8,128)(2,1)S(1)} %get-tuple-element.7.right, s32[32]{0:T(128)S(1)} %copy-done.3), custom_call_target="tpu_custom_call" | custom-call | tf_op jit(solution)/shard_map/pallas_call | solution.py:491
Async XLA Ops:
  0.6 1.6 %copy-start = (f32[512,1024]{1,0:T(8,128)S(1)}, f32[512,1024]{1,0:T(8,128)}, u32[]{:S(2)}) copy-start(f32[512,1024]{1,0:T(8,128)} %front.3) | copy-start | bytes 6291460
  2.2 0.7 copy-start.1
  2.9 0.7 copy-start.2
  3.6 0.7 copy-start.3

commit v3 on v2

--- a/solution.py
+++ b/solution.py
@@ -11,8 +11,7 @@
 NP = 2
 TS = 128
 MT = 512
-NB = 32
-SUB = 8
+NB = 64
 F32 = jnp.float32
 BF16 = jnp.bfloat16
 MESH = pl.DeviceIdType.MESH
@@ -46,45 +45,59 @@
 
 
 def block_inverse(block):
-    ii = lax.broadcasted_iota(jnp.int32, (NB, 128), 0)
-    ll = lax.broadcasted_iota(jnp.int32, (NB, 128), 1)
-    m = jnp.where(ll < NB, block, jnp.where(ll == ii + NB, 1.0, 0.0).astype(F32))
-    done = []
-    for g in range(NB // SUB):
-        low = SUB * g
-        rows = [m[low + i : low + i + 1, :] for i in range(SUB)]
+    ii = lax.broadcasted_iota(jnp.int32, (8, 128), 0)
+    ll = lax.broadcasted_iota(jnp.int32, (8, 128), 1)
+    groups = NB // 8
+    m = []
+    for g in range(groups):
+        unit = jnp.where(ll == ii + (8 * g + NB), 1.0, 0.0).astype(F32)
+        m.append(jnp.where(ll < NB, block[8 * g : 8 * g + 8, :], unit))
+    for g in range(groups):
+        low = 8 * g
+        rest = range(g + 1, groups)
+        rows = [jnp.broadcast_to(m[g][i : i + 1, :], (8, 128)) for i in range(8)]
         s = {}
-        for i in range(SUB):
-            for k in range(i, SUB):
-                s[i, k] = jnp.broadcast_to(rows[i][:, low + k : low + k + 1], (1, 128))
-        for j in range(SUB):
+        for i in range(8):
+            for k in range(i, 8):
+                s[i, k] = jnp.broadcast_to(rows[i][:, low + k : low + k + 1], (8, 128))
+        cols = {}
+        for h in rest:
+            for k in range(8):
+                cols[h, k] = jnp.broadcast_to(m[h][:, low + k : low + k + 1], (8, 128))
+        for j in range(8):
             inv = lax.rsqrt(s[j, j])
-            for k in range(j, SUB):
+            for k in range(j + 1, 8):
                 s[j, k] = s[j, k] * inv
+            for i in range(j + 1, 8):
+                for k in range(i, 8):
+                    s[i, k] = s[i, k] - s[j, i] * s[j, k]
             rows[j] = rows[j] * inv
-            for i in range(j + 1, SUB):
-                for k in range(i, SUB):
-                    s[i, k] = s[i, k] - s[j, i] * s[j, k]
+            for i in range(j + 1, 8):
                 rows[i] = rows[i] - s[j, i] * rows[j]
-        upper = jnp.concatenate(rows, axis=0)
-        done.append(upper)
-        if low + SUB < NB:
-            across = jnp.transpose(jnp.concatenate([upper] * (128 // SUB), axis=0))
-            for j in range(SUB):
-                column = jnp.where(ii[:, 0:1] >= low + SUB, across[:NB, j : j + 1], 0.0)
-                m = m - column * rows[j]
-    return jnp.concatenate(done, axis=0)[:, NB : 2 * NB]
+            for h in rest:
+                cols[h, j] = cols[h, j] * inv
+                for i in range(j + 1, 8):
+                    cols[h, i] = cols[h, i] - s[j, i] * cols[h, j]
+        merged = rows[0]
+        for i in range(1, 8):
+            merged = jnp.where(ii == i, rows[i], merged)
+        m[g] = merged
+        for h in rest:
+            for j in range(8):
+                m[h] = m[h] - cols[h, j] * rows[j]
+    return jnp.concatenate(m, axis=0)[:, NB : 2 * NB]
 
 
 def factor(work, beside):
     lane = lax.broadcasted_iota(jnp.int32, (NB, PW), 1)
 
     def step(b):
-        beside(b)
+        beside(2 * b)
         here = pl.ds(pl.multiple_of(b * NB, NB), NB)
         band = work[here, :]
         lead = pltpu.roll(band[:, :PW], PW - b * NB, axis=1)
         inverse = block_inverse(lead[:, :128])
+        beside(2 * b + 1)
         upper = dot6(inverse, band, 1, 0)
         below = jnp.where(lane >= (b + 1) * NB, upper[:, :PW], 0.0)
         work[...] -= dot6(below, upper, 0, 0)
@@ -110,8 +123,9 @@
 
 
 def front_kernel(
-    front, child, groups, tile_map, map_lanes,
+    front_hbm, child_hbm, groups_hbm, map_hbm, lanes_hbm,
     out_a, out_b,
+    fcols, frows, child, groups, tile_map, map_lanes, in_s,
     zin, srow, zbuf, partner, placed, dpiece, vpiece,
     diag, vpiv, strip_r, strip_c, v_r, v_c, flags,
     work, wp, x0, x1, p01,
@@ -122,7 +136,7 @@
     c = lax.axis_index("col")
     rows = lax.axis_size("row")
     cols = lax.axis_size("col")
-    height, width = front.shape
+    height, width = front_hbm.shape
     z = r // 2
     core = r % 2
     chips = rows // 2
@@ -133,14 +147,27 @@
 
     barrier = pltpu.get_barrier_semaphore()
 
-    def hello_row(i):
-        pl.semaphore_signal(barrier, inc=1, device_id=(lax.rem(r + i + 1, rows), c), device_id_type=MESH)
-
-    def hello_col(i):
-        pl.semaphore_signal(barrier, inc=1, device_id=(r, lax.rem(c + i + 1, cols)), device_id_type=MESH)
-
-    loop(rows - 1, hello_row)
-    loop(cols - 1, hello_col)
+    loads = [
+        pltpu.make_async_copy(src, dst, in_s.at[i])
+        for i, (src, dst) in enumerate([
+            (front_hbm.at[:, pl.ds(0, 128)], fcols.at[0]),
+            (front_hbm.at[:, pl.ds(MT, 128)], fcols.at[1]),
+            (child_hbm, child),
+            (groups_hbm, groups),
+            (map_hbm, tile_map),
+            (front_hbm.at[pl.ds(0, 16), :], frows),
+            (lanes_hbm, map_lanes),
+        ])
+    ]
+    for load in loads:
+        load.start()
+
+    def hello(row, col):
+        pl.semaphore_signal(barrier, inc=1, device_id=(row, col), device_id_type=MESH)
+
+    loop(chips - 1, lambda i: hello(lax.rem(r + 2 * i + 2, rows), c))
+    loop(cols - 1, lambda i: hello(r, lax.rem(c + i + 1, cols)))
+    hello(2 * z + 1 - core, c)
 
     @pl.when(jnp.logical_not(t_self))
     def _():
@@ -149,10 +176,13 @@
     def one_if(same):
         return jnp.where(same, 1.0, 0.0).astype(F32)
 
+    for load in loads:
+        load.wait()
+
     coupled = [one_if(groups[r] == groups[2 * c + q]) for q in range(2)]
     turned = []
     for q in range(2):
-        t = jnp.transpose(front[:, q * MT : q * MT + 128])[:16] * coupled[q]
+        t = jnp.transpose(fcols[q])[:16] * coupled[q]
         srow[0, 8 * q : 8 * q + 8, :] = t[:8]
         srow[1, 8 * q : 8 * q + 8, :] = t[8:]
         turned.append(t[:, :128])
@@ -178,29 +208,91 @@
     )
     zin[...] = jnp.transpose(tall)[:8]
 
-    pl.semaphore_wait(barrier, rows + cols - 2 + jnp.where(t_self, 0, 1))
+    pl.semaphore_wait(barrier, chips + cols - 1 + jnp.where(t_self, 0, 1))
 
     def z_copy(i):
         return pltpu.make_async_remote_copy(
-            src_ref=zin, dst_ref=zbuf.at[r], send_sem=z_s.at[i], recv_sem=z_r.at[i],
-            device_id=(lax.rem(r + i + 1, rows), c), device_id_type=MESH)
+            src_ref=zin, dst_ref=zbuf.at[core, z], send_sem=z_s.at[i], recv_sem=z_r.at[i],
+            device_id=(lax.rem(r + 2 * i + 2, rows), c), device_id_type=MESH)
+
+    def share_copy():
+        return pltpu.make_async_remote_copy(
+            src_ref=zbuf.at[core], dst_ref=zbuf.at[core],
+            send_sem=z_s.at[chips - 1], recv_sem=z_r.at[chips - 1],
+            device_id=(2 * z + 1 - core, c), device_id_type=MESH)
 
     def partner_copy():
         return pltpu.make_async_remote_copy(
             src_ref=child, dst_ref=partner, send_sem=p_s, recv_sem=p_r,
             device_id=(other, c), device_id_type=MESH)
 
-    loop(rows - 1, lambda i: z_copy(i).start())
+    loop(chips - 1, lambda i: z_copy(i).start())
     partner_copy().start()
-    zbuf[pl.ds(r, 1)] = zin[...][None]
+    zbuf[core, pl.ds(z, 1)] = zin[...][None]
 
     own8 = pl.ds(pl.multiple_of(r * 8, 8), 8)
     own16 = pl.ds(pl.multiple_of(c * 16, 16), 16)
     for k in range(2):
         for q in range(2):
             strip_c[k, own8, q * MT : (q + 1) * MT] = (
-                front[8 * k : 8 * k + 8, q * MT : (q + 1) * MT] * coupled[q])
+                frows[8 * k : 8 * k + 8, q * MT : (q + 1) * MT] * coupled[q])
     strip_r[:, own16, :] = srow[...]
+
+    def slot(shift):
+        return lax.rem(z + shift + chips, chips) * 2 + core
+
+    def piece(a, row):
+        if a == 0:
+            return strip_c.at[:, pl.ds(pl.multiple_of(row * 8, 8), 8), :]
+        return v_c.at[row]
+
+    def ring_copy(a, way, s):
+        sign = 1 - 2 * way
+        ref = piece(a, slot(-sign * s))
+        return pltpu.make_async_remote_copy(
+            src_ref=ref, dst_ref=ref, send_sem=ring_s.at[a, way, s], recv_sem=ring_r.at[a, way, s],
+            device_id=(slot(sign), c), device_id_type=MESH)
+
+    def sib_copy(a, row):
+        ref = piece(a, row)
+        return pltpu.make_async_remote_copy(
+            src_ref=ref, dst_ref=ref, send_sem=sib_s.at[a, row // 2], recv_sem=sib_r.at[a, row // 2],
+            device_id=(2 * z + 1 - core, c), device_id_type=MESH)
+
+    hops = chips // 2
+
+    def ring_start(a, s):
+        ring_copy(a, 0, s).start()
+
+        @pl.when(s < hops - 1)
+        def _():
+            ring_copy(a, 1, s).start()
+
+        sib_copy(a, slot(-s)).start()
+
+        @pl.when(s > 0)
+        def _():
+            sib_copy(a, slot(s)).start()
+
+    def ring_wait(a, s):
+        ring_copy(a, 0, s).wait_recv()
+
+        @pl.when(s < hops - 1)
+        def _():
+            ring_copy(a, 1, s).wait_recv()
+
+    def ring_next(a, s):
+        ring_wait(a, s)
+
+        @pl.when(s < hops - 1)
+        def _():
+            ring_start(a, s + 1)
+
+        @pl.when(s == hops - 1)
+        def _():
+            sib_copy(a, slot(hops)).start()
+
+    ring_start(0, 0)
 
     listed = jnp.transpose(jnp.broadcast_to(map_lanes[...].astype(F32), (128, 128)))
     count = map_lanes.shape[1]
@@ -239,8 +331,12 @@
     def vr_copy(i):
         return plane_copy(3, placed, v_r.at[own16, :], i)
 
-    loop(rows - 1, lambda i: z_copy(i).wait_recv())
-    flat = jnp.transpose(zbuf[...].reshape(rows * 8, 128))
+    loop(chips - 1, lambda i: z_copy(i).wait_recv())
+    share_copy().start()
+    ring_next(0, 0)
+    share_copy().wait_recv()
+    flat = jnp.transpose(
+        jnp.concatenate([zbuf[i % 2, i // 2] for i in range(rows)], axis=0))
     dpiece[0] = flat[0:16]
     dpiece[1] = flat[16:32]
     dpiece[2] = flat[32:48]
@@ -283,68 +379,25 @@
     loop(cols - 1, lambda i: vr_copy(i).start())
     loop(cols - 1, lambda i: sr_copy(i).start())
 
+    ring_next(0, 1)
+
     @pl.when(jnp.logical_not(t_self))
     def _():
         t_copy().wait_recv()
 
-    def slot(shift):
-        return lax.rem(z + shift + chips, chips) * 2 + core
-
-    def piece(a, row):
-        if a == 0:
-            return strip_c.at[:, pl.ds(pl.multiple_of(row * 8, 8), 8), :]
-        return v_c.at[row]
-
-    def ring_copy(a, way, s):
-        sign = 1 - 2 * way
-        ref = piece(a, slot(-sign * s))
-        return pltpu.make_async_remote_copy(
-            src_ref=ref, dst_ref=ref, send_sem=ring_s.at[a, way, s], recv_sem=ring_r.at[a, way, s],
-            device_id=(slot(sign), c), device_id_type=MESH)
-
-    def sib_copy(a, row):
-        ref = piece(a, row)
-        return pltpu.make_async_remote_copy(
-            src_ref=ref, dst_ref=ref, send_sem=sib_s.at[a, row // 2], recv_sem=sib_r.at[a, row // 2],
-            device_id=(2 * z + 1 - core, c), device_id_type=MESH)
-
-    hops = chips // 2
-
-    def ring_start(s):
-        for a in range(2):
-            ring_copy(a, 0, s).start()
-
-            @pl.when(s < hops - 1)
-            def _():
-                ring_copy(a, 1, s).start()
-
-            sib_copy(a, slot(-s)).start()
-
-            @pl.when(s > 0)
-            def _():
-                sib_copy(a, slot(s)).start()
-
-    def ring_wait(s):
-        for a in range(2):
-            ring_copy(a, 0, s).wait_recv()
-
-            @pl.when(s < hops - 1)
-            def _():
-                ring_copy(a, 1, s).wait_recv()
-
-    ring_start(0)
+    ring_start(1, 0)
 
     def ring_beside(first):
         def beside(b):
-            s = first + b // 2
-
-            @pl.when(b % 2 == 1)
+            t = first + b // 2
+
+            @pl.when(jnp.logical_and(b % 2 == 1, t < hops - 2))
             def _():
-                ring_wait(s)
-
-                @pl.when(s < hops - 1)
-                def _():
-                    ring_start(s + 1)
+                ring_next(0, t + 2)
+
+            @pl.when(jnp.logical_and(b % 2 == 0, t > 0))
+            def _():
+                ring_next(1, t - 1)
 
         return beside
 
@@ -370,8 +423,7 @@
     work[:, PW:] = eye
     factor(work, ring_beside(hops // 2))
     x1[...] = left3(work[:, PW:])
-    for a in range(2):
-        sib_copy(a, slot(hops)).start()
+    ring_next(1, hops - 1)
 
     for copy in (sr_copy, vr_copy):
         loop(cols - 1, lambda i: copy(i).wait_recv())
@@ -403,7 +455,8 @@
             lanes = slice(height + at.start, height + at.stop)
             tile(strip_c, v, flags[0:1, lanes], out_b, at, BF16(-1))
 
-    loop(rows - 1, lambda i: z_copy(i).wait_send())
+    loop(chips - 1, lambda i: z_copy(i).wait_send())
+    share_copy().wait_send()
     partner_copy().wait_send()
 
     @pl.when(jnp.logical_not(t_self))
@@ -420,19 +473,25 @@
 
 def panels(front, child, tile_group, row_map, rows, cols):
     vmem = pl.BlockSpec(memory_space=pltpu.VMEM)
-    smem = pl.BlockSpec(memory_space=pltpu.SMEM)
     dma = pltpu.SemaphoreType.DMA
     shape = jax.ShapeDtypeStruct
     height, width = front.shape
     return pl.pallas_call(
         front_kernel,
         out_shape=(shape((4 * PW, height), BF16), shape((4 * PW, width), BF16)),
-        in_specs=[vmem, vmem, smem, smem, vmem],
+        in_specs=[pl.BlockSpec(memory_space=pltpu.HBM)] * 5,
         out_specs=(vmem, vmem),
         scratch_shapes=[
+            pltpu.VMEM((2, height, 128), F32),
+            pltpu.VMEM((16, width), F32),
+            pltpu.VMEM((16, height), BF16),
+            pltpu.SMEM(tile_group.shape, jnp.int32),
+            pltpu.SMEM(row_map.shape, jnp.int32),
+            pltpu.VMEM((1, row_map.shape[0]), jnp.int32),
+            dma((7,)),
             pltpu.VMEM((8, 128), F32),
             pltpu.VMEM((2, 16, height), F32),
-            pltpu.VMEM((rows, 8, 128), F32),
+            pltpu.VMEM((2, rows // 2, 8, 128), F32),
             pltpu.VMEM((16, height), BF16),
             pltpu.VMEM((16, height), BF16),
             pltpu.VMEM((3, 16, PW), F32),
@@ -449,63 +508,65 @@
             pltpu.VMEM((PW, 3 * PW), BF16),
             pltpu.VMEM((PW, 3 * PW), BF16),
             pltpu.VMEM((PW, PW), BF16),
-            dma((rows - 1,)), dma((rows - 1,)), dma, dma, dma, dma,
+            dma((rows // 2,)), dma((rows // 2,)), dma, dma, dma, dma,
             dma((5, cols - 1)), dma((5, cols - 1)),
             dma((2, 2, rows // 4)), dma((2, 2, rows // 4)),
             dma((2, rows // 2)), dma((2, rows // 2)),
         ],
         compiler_params=pltpu.CompilerParams(
             collective_id=0, has_side_effects=True, vmem_limit_bytes=40 << 20),
-    )(front, child, tile_group, row_map, row_map.reshape(1, -1))
-
-
-def final_kernel(front, left, right, groups, schur, panel):
-    g = pl.program_id(0)
+    )(*(
+        pltpu.with_memory_space_constraint(x, pltpu.HBM)
+        for x in (front, child, tile_group, row_map, row_map.reshape(1, -1))))
+
+
+def final_kernel(front, left, right, groups, schur_hbm, panel, done, sem):
     r = lax.axis_index("row")
     c = lax.axis_index("col")
-    rows, wide = schur.shape
+    rows, width = front.shape
+    wide = done.shape[2]
     ii = lax.broadcasted_iota(jnp.int32, (rows, wide), 0)
-    jj = lax.rem(lax.broadcasted_iota(jnp.int32, (rows, wide), 1) + g * wide, MT)
-    keep = jnp.logical_and(ii >= 16, jj >= 16)
-    coupled = jnp.where(groups[r] == groups[2 * c + (g * wide) // MT], 1.0, 0.0).astype(F32)
-    total = front[...] * coupled + dot1(left[...], right[...], 0, 0)
-    schur[...] = jnp.where(keep, total, 0.0)
-
-    @pl.when(g == 0)
-    def _():
-        at = pl.multiple_of(c * 16, 16)
-        m = lax.broadcasted_iota(jnp.int32, (16, rows), 0) + c * 16
-        a = lax.broadcasted_iota(jnp.int32, (16, rows), 1)
-        p0 = left[pl.ds(2 * PW + at, 16), :].astype(F32)
-        p1 = left[pl.ds(3 * PW + at, 16), :].astype(F32)
-        p0 = jnp.where(jnp.logical_or(a >= 8, m <= r * 8 + a), p0, 0.0)
-        p1 = jnp.where(jnp.logical_or(a >= 16, m <= r * 8 + a - 8), p1, 0.0)
-        p1 = jnp.where(a >= 8, p1, 0.0)
-        panel[0:16, :] = p0.astype(BF16)
-        panel[16:32, :] = p1.astype(BF16)
+    jj = lax.broadcasted_iota(jnp.int32, (rows, wide), 1)
+    copies = []
+    for g in range(width // wide):
+        at = slice(g * wide, (g + 1) * wide)
+        keep = jnp.logical_and(ii >= 16, lax.rem(jj + g * wide, MT) >= 16)
+        coupled = jnp.where(groups[r] == groups[2 * c + (g * wide) // MT], 1.0, 0.0).astype(F32)
+        total = front[:, at] * coupled + dot1(left[...], right[:, at], 0, 0)
+        done[g] = jnp.where(keep, total, 0.0)
+        copies.append(pltpu.make_async_copy(done.at[g], schur_hbm.at[:, pl.ds(g * wide, wide)], sem.at[g]))
+        copies[-1].start()
+    at = pl.multiple_of(c * 16, 16)
+    m = lax.broadcasted_iota(jnp.int32, (16, rows), 0) + c * 16
+    a = lax.broadcasted_iota(jnp.int32, (16, rows), 1)
+    p0 = left[pl.ds(2 * PW + at, 16), :].astype(F32)
+    p1 = left[pl.ds(3 * PW + at, 16), :].astype(F32)
+    p0 = jnp.where(jnp.logical_or(a >= 8, m <= r * 8 + a), p0, 0.0)
+    p1 = jnp.where(jnp.logical_or(a >= 16, m <= r * 8 + a - 8), p1, 0.0)
+    p1 = jnp.where(a >= 8, p1, 0.0)
+    panel[0:16, :] = p0.astype(BF16)
+    panel[16:32, :] = p1.astype(BF16)
+    for copy in copies:
+        copy.wait()
 
 
 def final(front, left, right, tile_group):
-    rows, wide = front.shape
+    rows, width = front.shape
     step = 256
+    vmem = pl.BlockSpec(memory_space=pltpu.VMEM)
     return pl.pallas_call(
         final_kernel,
-        grid=(wide // step,),
         out_shape=(
-            jax.ShapeDtypeStruct((rows, wide), F32),
+            jax.ShapeDtypeStruct((rows, width), F32),
             jax.ShapeDtypeStruct((32, rows), BF16),
         ),
-        in_specs=[
-            pl.BlockSpec((rows, step), lambda g: (0, g)),
-            pl.BlockSpec((4 * PW, rows), lambda g: (0, 0)),
-            pl.BlockSpec((4 * PW, step), lambda g: (0, g)),
-            pl.BlockSpec(memory_space=pltpu.SMEM),
+        in_specs=[vmem, vmem, vmem, pl.BlockSpec(memory_space=pltpu.SMEM)],
+        out_specs=(pl.BlockSpec(memory_space=pltpu.HBM), vmem),
+        scratch_shapes=[
+            pltpu.VMEM((width // step, rows, step), F32),
+            pltpu.SemaphoreType.DMA((width // step,)),
         ],
-        out_specs=(
-            pl.BlockSpec((rows, step), lambda g: (0, g)),
-            pl.BlockSpec((32, rows), lambda g: (0, 0)),
-        ),
-        compiler_params=pltpu.CompilerParams(vmem_limit_bytes=32 << 20),
+        compiler_params=pltpu.CompilerParams(vmem_limit_bytes=16 << 20),
     )(front, left, right, tile_group)
 
 

time: 92.3 us -> 80.5 us (0.87)
  the two profiles are of different devices: /device:TPU:4 before, /device:TPU:6 now
where the time goes in v3:
time: 80.5 us; the launch traced here: 80.4 us
  Pallas kernels  79.7 us (99%)
    pallas_call x1, Pallas kernels, panels(): pl.pallas_call(front_kernel, out_shape=(shape((4 * PW, height), BF16), sh...  76.2 us
    pallas_call x1, Pallas kernels, final(): pl.pallas_call(final_kernel, out_shape=(jax.ShapeDtypeStruct((rows, width...  3.5 us

profile of v3, /device:TPU:6, one launch (start us, length us, event | category | flops | bytes accessed | tf_op | source)
XLA Modules:
  0.0 80.4 jit_solution(13061001359884801107)
XLA Ops:
  0.6 0.0 copy-start.1
  0.6 0.0 copy-start
  0.7 76.2 %shard_map.59 = (bf16[1024,512]{1,0:T(8,128)(2,1)S(1)}, bf16[1024,1024]{1,0:T(8,128)(2,1)S(1)}) custom-call(f32[512,1024]{1,0:T(8,128)} %front.1, bf16[16,512]{1,0:T(8,128)(2,1)} %bitcast.3, s32[32]{0:T(128)} %groups.1, s32[128]{0:T(128)} %map_hbm.1, s32[1,128]{1,0:T(1,128)} %bitcast.4), custom_call_target="tpu_custom_call" | custom-call | tf_op jit(solution)/shard_map/pallas_call | solution.py:479
  76.8 0.0 copy-done.1
  76.9 0.0 copy-done
  76.9 3.5 %shard_map.60 = (f32[512,1024]{1,0:T(8,128)}, bf16[32,512]{1,0:T(8,128)(2,1)}) custom-call(f32[512,1024]{1,0:T(8,128)S(1)} %copy-done, bf16[1024,512]{1,0:T(8,128)(2,1)S(1)} %get-tuple-element.6.left, bf16[1024,1024]{1,0:T(8,128)(2,1)S(1)} %get-tuple-element.7.right, s32[32]{0:T(128)S(1)} %copy-done.1), custom_call_target="tpu_custom_call" | custom-call | tf_op jit(solution)/shard_map/pallas_call | solution.py:557
Async XLA Ops:
  0.6 76.2 %copy-start.1 = (s32[32]{0:T(128)S(1)}, s32[32]{0:T(128)}, u32[]{:S(2)}) copy-start(s32[32]{0:T(128)} %groups.1) | copy-start | bytes 388
  0.6 76.2 %copy-start = (f32[512,1024]{1,0:T(8,128)S(1)}, f32[512,1024]{1,0:T(8,128)}, u32[]{:S(2)}) copy-start(f32[512,1024]{1,0:T(8,128)} %front.1) | copy-start | bytes 6291460

commit v4 on v3

--- a/solution.py
+++ b/solution.py
@@ -88,22 +88,19 @@
     return jnp.concatenate(m, axis=0)[:, NB : 2 * NB]
 
 
-def factor(work, beside):
+def factor_step(work, b, beside, extra):
     lane = lax.broadcasted_iota(jnp.int32, (NB, PW), 1)
-
-    def step(b):
-        beside(2 * b)
-        here = pl.ds(pl.multiple_of(b * NB, NB), NB)
-        band = work[here, :]
-        lead = pltpu.roll(band[:, :PW], PW - b * NB, axis=1)
-        inverse = block_inverse(lead[:, :128])
-        beside(2 * b + 1)
-        upper = dot6(inverse, band, 1, 0)
-        below = jnp.where(lane >= (b + 1) * NB, upper[:, :PW], 0.0)
-        work[...] -= dot6(below, upper, 0, 0)
-        work[here, :] = upper
-
-    loop(PW // NB, step)
+    beside(2 * b)
+    here = pl.ds(pl.multiple_of(b * NB, NB), NB)
+    band = work[here, :]
+    lead = pltpu.roll(band[:, :PW], (PW - b * NB) % PW, axis=1)
+    inverse = block_inverse(lead[:, :128])
+    beside(2 * b + 1)
+    extra(b)
+    upper = dot6(inverse, band, 1, 0)
+    below = jnp.where(lane >= (b + 1) * NB, upper[:, :PW], 0.0)
+    work[...] -= dot6(below, upper, 0, 0)
+    work[here, :] = upper
 
 
 def split2(x, axis):
@@ -124,13 +121,13 @@
 
 def front_kernel(
     front_hbm, child_hbm, groups_hbm, map_hbm, lanes_hbm,
-    out_a, out_b,
+    out_a, out_b, own_p,
     fcols, frows, child, groups, tile_map, map_lanes, in_s,
     zin, srow, zbuf, partner, placed, dpiece, vpiece,
     diag, vpiv, strip_r, strip_c, v_r, v_c, flags,
-    work, wp, x0, x1, p01,
+    work, wp, x0, x1, p01, turned_r, later,
     z_s, z_r, p_s, p_r, t_s, t_r,
-    plane_s, plane_r, ring_s, ring_r, sib_s, sib_r,
+    plane_s, plane_r, ring_s, ring_r, sib_s, sib_r, d_s, d_r,
 ):
     r = lax.axis_index("row")
     c = lax.axis_index("col")
@@ -294,23 +291,6 @@
 
     ring_start(0, 0)
 
-    listed = jnp.transpose(jnp.broadcast_to(map_lanes[...].astype(F32), (128, 128)))
-    count = map_lanes.shape[1]
-    at_lane = lax.broadcasted_iota(jnp.int32, (128, 128), 1).astype(F32)
-    child_id = lax.broadcasted_iota(jnp.int32, (128, 128), 0)
-    hits = jnp.where(jnp.logical_and(listed == at_lane, child_id >= count // 2), 1.0, 0.0)
-    second = jnp.broadcast_to(jnp.sum(hits, axis=0, keepdims=True), (8, 128)).astype(BF16)
-
-    def spread(tile_of_lane, lanes):
-        tile = lax.broadcasted_iota(jnp.int32, (128, lanes), 0)
-        lane = lax.broadcasted_iota(jnp.int32, (128, lanes), 1)
-        chosen = jnp.where(tile == tile_of_lane(lane), 1.0, 0.0).astype(BF16)
-        return dot1(second, chosen, 1, 0).astype(BF16)
-
-    flag_p = spread(lambda lane: 4 * lax.shift_right_logical(lane, 3), PW)[0:1]
-    flags[0:8, :height] = spread(lambda lane: 4 * r + lax.shift_right_logical(lane, 7), height).astype(F32)
-    flags[0:8, height:] = spread(lambda lane: 8 * c + lax.shift_right_logical(lane, 7), width).astype(F32)
-
     def plane_copy(a, src, dst, i):
         return pltpu.make_async_remote_copy(
             src_ref=src, dst_ref=dst, send_sem=plane_s.at[a, i], recv_sem=plane_r.at[a, i],
@@ -323,7 +303,12 @@
         return plane_copy(1, dpiece.at[0], diag.at[0, own16, :], i)
 
     def d1_copy(i):
-        return plane_copy(4, dpiece.at[pl.ds(1, 2)], diag.at[pl.ds(1, 2), own16, :], i)
+        return plane_copy(4, dpiece.at[1 + core], diag.at[1 + core, own16, :], i)
+
+    def d1_share():
+        return pltpu.make_async_remote_copy(
+            src_ref=diag.at[1 + core], dst_ref=diag.at[1 + core], send_sem=d_s, recv_sem=d_r,
+            device_id=(2 * z + 1 - core, c), device_id_type=MESH)
 
     def vp_copy(i):
         return plane_copy(2, vpiece, vpiv.at[:, own16, :], i)
@@ -331,27 +316,7 @@
     def vr_copy(i):
         return plane_copy(3, placed, v_r.at[own16, :], i)
 
-    loop(chips - 1, lambda i: z_copy(i).wait_recv())
-    share_copy().start()
     ring_next(0, 0)
-    share_copy().wait_recv()
-    flat = jnp.transpose(
-        jnp.concatenate([zbuf[i % 2, i // 2] for i in range(rows)], axis=0))
-    dpiece[0] = flat[0:16]
-    dpiece[1] = flat[16:32]
-    dpiece[2] = flat[32:48]
-    half = rows * 4
-
-    def swapped_halves(x):
-        return jnp.concatenate([x[:, half:], x[:, :half]], axis=1)
-
-    vpiece[0] = (flat[64:80] + swapped_halves(flat[80:96])).astype(BF16)
-    vpiece[1] = (flat[96:112] + swapped_halves(flat[112:128])).astype(BF16)
-    diag[:, own16, :] = dpiece[...]
-    vpiv[:, own16, :] = vpiece[...]
-    loop(cols - 1, lambda i: vp_copy(i).start())
-    loop(cols - 1, lambda i: d_copy(i).start())
-    loop(cols - 1, lambda i: d1_copy(i).start())
 
     partner_copy().wait_recv()
     for j in range(height // TS):
@@ -376,30 +341,58 @@
     def _():
         t_copy().start()
 
+    loop(chips - 1, lambda i: z_copy(i).wait_recv())
+    share_copy().start()
+    ring_next(0, 1)
+    share_copy().wait_recv()
+    flat = jnp.transpose(
+        jnp.concatenate([zbuf[i % 2, i // 2] for i in range(rows)], axis=0))
+    dpiece[0] = flat[0:16]
+    dpiece[1] = flat[16:32]
+    dpiece[2] = flat[32:48]
+    half = rows * 4
+
+    def swapped_halves(x):
+        return jnp.concatenate([x[:, half:], x[:, :half]], axis=1)
+
+    vpiece[0] = (flat[64:80] + swapped_halves(flat[80:96])).astype(BF16)
+    vpiece[1] = (flat[96:112] + swapped_halves(flat[112:128])).astype(BF16)
+    diag[0, own16, :] = dpiece[0]
+    diag[1 + core, own16, :] = dpiece[1 + core]
+    vpiv[:, own16, :] = vpiece[...]
+    loop(cols - 1, lambda i: vp_copy(i).start())
+    loop(cols - 1, lambda i: d_copy(i).start())
+    loop(cols - 1, lambda i: d1_copy(i).start())
+
     loop(cols - 1, lambda i: vr_copy(i).start())
     loop(cols - 1, lambda i: sr_copy(i).start())
-
-    ring_next(0, 1)
 
     @pl.when(jnp.logical_not(t_self))
     def _():
         t_copy().wait_recv()
 
     ring_start(1, 0)
-
-    def ring_beside(first):
-        def beside(b):
-            t = first + b // 2
-
-            @pl.when(jnp.logical_and(b % 2 == 1, t < hops - 2))
-            def _():
-                ring_next(0, t + 2)
-
-            @pl.when(jnp.logical_and(b % 2 == 0, t > 0))
-            def _():
-                ring_next(1, t - 1)
-
-        return beside
+    ring_next(0, 2)
+
+    listed = jnp.transpose(jnp.broadcast_to(map_lanes[...].astype(F32), (128, 128)))
+    count = map_lanes.shape[1]
+    at_lane = lax.broadcasted_iota(jnp.int32, (128, 128), 1).astype(F32)
+    child_id = lax.broadcasted_iota(jnp.int32, (128, 128), 0)
+    hits = jnp.where(jnp.logical_and(listed == at_lane, child_id >= count // 2), 1.0, 0.0)
+    second = jnp.broadcast_to(jnp.sum(hits, axis=0, keepdims=True), (8, 128)).astype(BF16)
+
+    def spread(tile_of_lane, lanes):
+        tile = lax.broadcasted_iota(jnp.int32, (128, lanes), 0)
+        lane = lax.broadcasted_iota(jnp.int32, (128, lanes), 1)
+        chosen = jnp.where(tile == tile_of_lane(lane), 1.0, 0.0).astype(BF16)
+        return dot1(second, chosen, 1, 0).astype(BF16)
+
+    flag_p = spread(lambda lane: 4 * lax.shift_right_logical(lane, 3), PW)[0:1]
+    flags[0:8, :height] = spread(lambda lane: 4 * r + lax.shift_right_logical(lane, 7), height).astype(F32)
+    flags[0:8, height:] = spread(lambda lane: 8 * c + lax.shift_right_logical(lane, 7), width).astype(F32)
+
+    ring_next(0, 3)
+    ring_next(1, 0)
 
     loop(cols - 1, lambda i: vp_copy(i).wait_recv())
     for k in range(2):
@@ -409,54 +402,105 @@
     i = lax.broadcasted_iota(jnp.int32, (PW, PW), 0)
     j = lax.broadcasted_iota(jnp.int32, (PW, PW), 1)
     eye = jnp.where(i == j, 1.0, 0.0).astype(F32)
-    outer = dot1(wp[0], wp[0], 0, 0)
+    work[:, :PW] = dot1(wp[0], wp[0], 0, 0)
+    work[:, PW:] = eye
+    ring_next(0, 4)
+    ring_next(1, 1)
     loop(cols - 1, lambda i: d_copy(i).wait_recv())
-    work[:, :PW] = diag[0] + outer
-    work[:, PW:] = eye
-    factor(work, ring_beside(0))
+    work[:, :PW] += diag[0]
+
+    def beside(t):
+        @pl.when(t == 1)
+        def _():
+            ring_next(0, 5)
+            ring_next(1, 2)
+
+        @pl.when(t == 3)
+        def _():
+            ring_next(0, 6)
+            ring_next(1, 3)
+
+        @pl.when(t == 5)
+        def _():
+            ring_next(0, 7)
+            ring_next(1, 4)
+            loop(cols - 1, lambda i: d1_copy(i).wait_recv())
+            d1_share().start()
+
+        @pl.when(t == 7)
+        def _():
+            ring_next(1, 5)
+
+    loop(PW // NB, lambda b: factor_step(work, b, beside, lambda b: None))
     x0[...] = left3(work[:, PW:])
-    loop(cols - 1, lambda i: d1_copy(i).wait_recv())
+    d1_share().wait_recv()
+    ring_next(1, 6)
     low = diag[1] + dot1(wp[1], wp[0], 0, 0)
     p01[...] = dot1(right3(low, 1), x0[...], 1, 1).astype(BF16)
 
     work[:, :PW] = diag[2] + dot1(wp[1], wp[1], 0, 0) - dot1(p01[...], p01[...], 1, 1)
     work[:, PW:] = eye
-    factor(work, ring_beside(hops // 2))
+
+    def first_part(strip, v, flag, at):
+        flag = flag.astype(BF16)
+        bottom = v * flag
+        w = jnp.concatenate([v - bottom, bottom], axis=0)
+        s0 = strip[0, :, at] + dot1(wp[0], w, 0, 0)
+        first = dot1(x0[...], right3(s0, 0), 1, 0).astype(BF16)
+        s1 = strip[1, :, at] + dot1(wp[1], w, 0, 0) - dot1(p01[...], first, 1, 0)
+        return w, first, right3(s1, 0)
+
+    def col_tile(q, h):
+        sub = slice(h * PW, (h + 1) * PW)
+        at = slice(q * height + h * PW, q * height + (h + 1) * PW)
+        v = jnp.concatenate([v_c[2 * i + q, :, sub] for i in range(chips)], axis=0)
+        flag = flags[0:1, height + at.start : height + at.stop]
+        w, first, rest = first_part(strip_c, v, flag, at)
+        out_b[0 : 2 * PW, at] = w
+        out_b[2 * PW : 3 * PW, at] = -first
+        later[:, at] = rest
+
+    tiles = [(q, h) for q in range(2) for h in range(height // PW)]
+
+    def beside_second(t):
+        if t == 2:
+            ring_next(1, 7)
+            for a in range(2):
+                loop(chips, lambda i: sib_copy(a, 2 * i + core).wait_recv())
+
+    def extra_second(b):
+        if b == 2:
+            col_tile(*tiles[0])
+            col_tile(*tiles[1])
+        if b == 3:
+            col_tile(*tiles[2])
+            col_tile(*tiles[3])
+
+    for b in range(PW // NB):
+        factor_step(work, b, beside_second, extra_second)
     x1[...] = left3(work[:, PW:])
-    ring_next(1, hops - 1)
+
+    for q, h in tiles:
+        at = slice(q * height + h * PW, q * height + (h + 1) * PW)
+        out_b[3 * PW : 4 * PW, at] = -dot1(x1[...], later[:, at], 1, 0).astype(BF16)
 
     for copy in (sr_copy, vr_copy):
         loop(cols - 1, lambda i: copy(i).wait_recv())
-
-    def tile(strip, v, flag, out, at, sign):
-        flag = flag.astype(BF16)
-        bottom = v * flag
-        top = v - bottom
-        out[0:PW, at] = top
-        out[PW : 2 * PW, at] = bottom
-        w = jnp.concatenate([top, bottom], axis=0)
-        s0 = strip[0, :, at] + dot1(wp[0], w, 0, 0)
-        first = dot1(x0[...], right3(s0, 0), 1, 0).astype(BF16)
-        out[2 * PW : 3 * PW, at] = first * sign
-        s1 = strip[1, :, at] + dot1(wp[1], w, 0, 0) - dot1(p01[...], first, 1, 0)
-        second = dot1(x1[...], right3(s1, 0), 1, 0).astype(BF16)
-        out[3 * PW : 4 * PW, at] = second * sign
-
     for h in range(height // PW):
         at = slice(h * PW, (h + 1) * PW)
-        tile(strip_r, v_r[:, at], flags[0:1, at], out_a, at, BF16(1))
-    for a in range(2):
-        loop(chips, lambda i: sib_copy(a, 2 * i + core).wait_recv())
-    for q in range(2):
-        for h in range(height // PW):
-            sub = slice(h * PW, (h + 1) * PW)
-            at = slice(q * height + h * PW, q * height + (h + 1) * PW)
-            v = jnp.concatenate([v_c[2 * i + q, :, sub] for i in range(chips)], axis=0)
-            lanes = slice(height + at.start, height + at.stop)
-            tile(strip_c, v, flags[0:1, lanes], out_b, at, BF16(-1))
+        w, first, rest = first_part(strip_r, v_r[:, at], flags[0:1, at], at)
+        second = dot1(x1[...], rest, 1, 0).astype(BF16)
+        turned_r[0:PW, at] = first
+        turned_r[PW:, at] = second
+        out_a[at, 0 : 2 * PW] = jnp.transpose(w)
+        out_a[at, 2 * PW : 3 * PW] = jnp.transpose(first)
+        out_a[at, 3 * PW : 4 * PW] = jnp.transpose(second)
+    own_p[0:16, :] = turned_r[own16, :]
+    own_p[16:32, :] = turned_r[pl.ds(pl.multiple_of(PW + c * 16, 16), 16), :]
 
     loop(chips - 1, lambda i: z_copy(i).wait_send())
     share_copy().wait_send()
+    d1_share().wait_send()
     partner_copy().wait_send()
 
     @pl.when(jnp.logical_not(t_self))
@@ -478,9 +522,10 @@
     height, width = front.shape
     return pl.pallas_call(
         front_kernel,
-        out_shape=(shape((4 * PW, height), BF16), shape((4 * PW, width), BF16)),
+        out_shape=(
+            shape((height, 4 * PW), BF16), shape((4 * PW, width), BF16), shape((32, height), BF16)),
         in_specs=[pl.BlockSpec(memory_space=pltpu.HBM)] * 5,
-        out_specs=(vmem, vmem),
+        out_specs=(vmem, vmem, vmem),
         scratch_shapes=[
             pltpu.VMEM((2, height, 128), F32),
             pltpu.VMEM((16, width), F32),
@@ -508,10 +553,12 @@
             pltpu.VMEM((PW, 3 * PW), BF16),
             pltpu.VMEM((PW, 3 * PW), BF16),
             pltpu.VMEM((PW, PW), BF16),
+            pltpu.VMEM((2 * PW, height), BF16),
+            pltpu.VMEM((3 * PW, width), BF16),
             dma((rows // 2,)), dma((rows // 2,)), dma, dma, dma, dma,
             dma((5, cols - 1)), dma((5, cols - 1)),
             dma((2, 2, rows // 4)), dma((2, 2, rows // 4)),
-            dma((2, rows // 2)), dma((2, rows // 2)),
+            dma((2, rows // 2)), dma((2, rows // 2)), dma, dma,
         ],
         compiler_params=pltpu.CompilerParams(
             collective_id=0, has_side_effects=True, vmem_limit_bytes=40 << 20),
@@ -520,7 +567,7 @@
         for x in (front, child, tile_group, row_map, row_map.reshape(1, -1))))
 
 
-def final_kernel(front, left, right, groups, schur_hbm, panel, done, sem):
+def final_kernel(front, left, right, own_p, groups, schur_hbm, panel, done, sem):
     r = lax.axis_index("row")
     c = lax.axis_index("col")
     rows, width = front.shape
@@ -532,15 +579,14 @@
         at = slice(g * wide, (g + 1) * wide)
         keep = jnp.logical_and(ii >= 16, lax.rem(jj + g * wide, MT) >= 16)
         coupled = jnp.where(groups[r] == groups[2 * c + (g * wide) // MT], 1.0, 0.0).astype(F32)
-        total = front[:, at] * coupled + dot1(left[...], right[:, at], 0, 0)
+        total = front[:, at] * coupled + dot1(left[...], right[:, at], 1, 0)
         done[g] = jnp.where(keep, total, 0.0)
         copies.append(pltpu.make_async_copy(done.at[g], schur_hbm.at[:, pl.ds(g * wide, wide)], sem.at[g]))
         copies[-1].start()
-    at = pl.multiple_of(c * 16, 16)
     m = lax.broadcasted_iota(jnp.int32, (16, rows), 0) + c * 16
     a = lax.broadcasted_iota(jnp.int32, (16, rows), 1)
-    p0 = left[pl.ds(2 * PW + at, 16), :].astype(F32)
-    p1 = left[pl.ds(3 * PW + at, 16), :].astype(F32)
+    p0 = own_p[0:16, :].astype(F32)
+    p1 = own_p[16:32, :].astype(F32)
     p0 = jnp.where(jnp.logical_or(a >= 8, m <= r * 8 + a), p0, 0.0)
     p1 = jnp.where(jnp.logical_or(a >= 16, m <= r * 8 + a - 8), p1, 0.0)
     p1 = jnp.where(a >= 8, p1, 0.0)
@@ -550,7 +596,7 @@
         copy.wait()
 
 
-def final(front, left, right, tile_group):
+def final(front, left, right, own_p, tile_group):
     rows, width = front.shape
     step = 256
     vmem = pl.BlockSpec(memory_space=pltpu.VMEM)
@@ -560,21 +606,21 @@
             jax.ShapeDtypeStruct((rows, width), F32),
             jax.ShapeDtypeStruct((32, rows), BF16),
         ),
-        in_specs=[vmem, vmem, vmem, pl.BlockSpec(memory_space=pltpu.SMEM)],
+        in_specs=[vmem, vmem, vmem, vmem, pl.BlockSpec(memory_space=pltpu.SMEM)],
         out_specs=(pl.BlockSpec(memory_space=pltpu.HBM), vmem),
         scratch_shapes=[
             pltpu.VMEM((width // step, rows, step), F32),
             pltpu.SemaphoreType.DMA((width // step,)),
         ],
         compiler_params=pltpu.CompilerParams(vmem_limit_bytes=16 << 20),
-    )(front, left, right, tile_group)
+    )(front, left, right, own_p, tile_group)
 
 
 def local(front, tile_group, child, row_map):
     rows = lax.axis_size("row")
     cols = lax.axis_size("col")
-    left, right = panels(front, child.T, tile_group, row_map, rows, cols)
-    schur, panel = final(front, left, right, tile_group)
+    left, right, own_p = panels(front, child.T, tile_group, row_map, rows, cols)
+    schur, panel = final(front, left, right, own_p, tile_group)
     return panel.T, schur
 
 

time: 80.5 us -> 87.5 us (1.087); the launches traced: 80.4 us -> 86.4 us
  Pallas kernels: 79.7 us -> 85.6 us
    pallas_call x1, Pallas kernels: 76.2 us -> 82.1 us  [panels(): pl.pallas_call(front_kernel, out_shape=(shape((height, 4 * PW), BF16), sh...]
where the time goes in v4:
time: 87.5 us; the launch traced here: 86.4 us
  Pallas kernels  85.6 us (98%)
    pallas_call x1, Pallas kernels, panels(): pl.pallas_call(front_kernel, out_shape=(shape((height, 4 * PW), BF16), sh...  82.1 us
    pallas_call x1, Pallas kernels, final(): pl.pallas_call(final_kernel, out_shape=(jax.ShapeDtypeStruct((rows, width...  3.48 us

profile of v4, /device:TPU:6, one launch (start us, length us, event | category | flops | bytes accessed | tf_op | source)
XLA Modules:
  0.0 86.4 jit_solution(18187114115552369688)
XLA Ops:
  0.6 0.0 copy-start.1
  0.6 0.0 copy-start
  0.7 82.1 %shard_map.59 = (bf16[512,1024]{1,0:T(8,128)(2,1)S(1)}, bf16[1024,1024]{1,0:T(8,128)(2,1)S(1)}, bf16[32,512]{1,0:T(8,128)(2,1)S(1)}) custom-call(f32[512,1024]{1,0:T(8,128)} %front.1, bf16[16,512]{1,0:T(8,128)(2,1)} %bitcast.3, s32[32]{0:T(128)} %groups.1, s32[128]{0:T(128)} %map_hbm.1, s32[1,128]{1,0:T(1,128)} %bitcast.4), custom_call_target="tpu_custom_call" | custom-call | tf_op jit(solution)/shard_map/pallas_call | solution.py:523
  82.8 0.0 copy-done.1
  82.8 0.0 copy-done
  82.8 3.5 %shard_map.60 = (f32[512,1024]{1,0:T(8,128)}, bf16[32,512]{1,0:T(8,128)(2,1)}) custom-call(f32[512,1024]{1,0:T(8,128)S(1)} %copy-done, bf16[512,1024]{1,0:T(8,128)(2,1)S(1)} %get-tuple-element.7.left, bf16[1024,1024]{1,0:T(8,128)(2,1)S(1)} %get-tuple-element.8.right, bf16[32,512]{1,0:T(8,128)(2,1)S(1)} %get-tuple-element.9.own_p, s32[32]{0:T(128)S(1)} %copy-done.1), custom_call_target="tpu_custom_call" | custom-call | tf_op jit(solution)/shard_map/pallas_call | solution.py:603
Async XLA Ops:
  0.6 82.1 %copy-start.1 = (s32[32]{0:T(128)S(1)}, s32[32]{0:T(128)}, u32[]{:S(2)}) copy-start(s32[32]{0:T(128)} %groups.1) | copy-start | bytes 388
  0.6 82.1 %copy-start = (f32[512,1024]{1,0:T(8,128)S(1)}, f32[512,1024]{1,0:T(8,128)}, u32[]{:S(2)}) copy-start(f32[512,1024]{1,0:T(8,128)} %front.1) | copy-start | bytes 6291460

commit v5 on v4

--- a/solution.py
+++ b/solution.py
@@ -227,28 +227,26 @@
     partner_copy().start()
     zbuf[core, pl.ds(z, 1)] = zin[...][None]
 
-    own8 = pl.ds(pl.multiple_of(r * 8, 8), 8)
     own16 = pl.ds(pl.multiple_of(c * 16, 16), 16)
-    for k in range(2):
-        for q in range(2):
-            strip_c[k, own8, q * MT : (q + 1) * MT] = (
-                frows[8 * k : 8 * k + 8, q * MT : (q + 1) * MT] * coupled[q])
+    for q in range(2):
+        at = slice(q * MT, (q + 1) * MT)
+        strip_c[pl.ds(r, 1), :, at] = (frows[:, at] * coupled[q]).astype(BF16)[None]
     strip_r[:, own16, :] = srow[...]
 
     def slot(shift):
         return lax.rem(z + shift + chips, chips) * 2 + core
 
     def piece(a, row):
-        if a == 0:
-            return strip_c.at[:, pl.ds(pl.multiple_of(row * 8, 8), 8), :]
-        return v_c.at[row]
-
-    def ring_copy(a, way, s):
+        return strip_c.at[row] if a == 0 else v_c.at[row]
+
+    def ring_copy(a, way, distance):
         sign = 1 - 2 * way
-        ref = piece(a, slot(-sign * s))
-        return pltpu.make_async_remote_copy(
-            src_ref=ref, dst_ref=ref, send_sem=ring_s.at[a, way, s], recv_sem=ring_r.at[a, way, s],
-            device_id=(slot(sign), c), device_id_type=MESH)
+        near = distance <= 2
+        ref = piece(a, slot(0) if near else slot(-sign * (distance - 2)))
+        return pltpu.make_async_remote_copy(
+            src_ref=ref, dst_ref=ref,
+            send_sem=ring_s.at[a, way, distance - 1], recv_sem=ring_r.at[a, way, distance - 1],
+            device_id=(slot(sign * (distance if near else 2)), c), device_id_type=MESH)
 
     def sib_copy(a, row):
         ref = piece(a, row)
@@ -258,38 +256,23 @@
 
     hops = chips // 2
 
-    def ring_start(a, s):
-        ring_copy(a, 0, s).start()
-
-        @pl.when(s < hops - 1)
-        def _():
-            ring_copy(a, 1, s).start()
-
-        sib_copy(a, slot(-s)).start()
-
-        @pl.when(s > 0)
-        def _():
-            sib_copy(a, slot(s)).start()
-
-    def ring_wait(a, s):
-        ring_copy(a, 0, s).wait_recv()
-
-        @pl.when(s < hops - 1)
-        def _():
-            ring_copy(a, 1, s).wait_recv()
-
-    def ring_next(a, s):
-        ring_wait(a, s)
-
-        @pl.when(s < hops - 1)
-        def _():
-            ring_start(a, s + 1)
-
-        @pl.when(s == hops - 1)
-        def _():
-            sib_copy(a, slot(hops)).start()
-
-    ring_start(0, 0)
+    def ring_pairs(stage):
+        return [(way, d) for d in (2 * stage + 1, 2 * stage + 2) for way in range(2) if d < hops or way == 0]
+
+    def ring_next(a, stage):
+        if stage == 0:
+            sib_copy(a, slot(0)).start()
+        else:
+            for way, d in ring_pairs(stage - 1):
+                ring_copy(a, way, d).wait_recv()
+        if stage < hops // 2:
+            for way, d in ring_pairs(stage):
+                ring_copy(a, way, d).start()
+        if stage > 0:
+            for way, d in ring_pairs(stage - 1):
+                sib_copy(a, slot(-(1 - 2 * way) * d)).start()
+
+    ring_next(0, 0)
 
     def plane_copy(a, src, dst, i):
         return pltpu.make_async_remote_copy(
@@ -315,8 +298,6 @@
 
     def vr_copy(i):
         return plane_copy(3, placed, v_r.at[own16, :], i)
-
-    ring_next(0, 0)
 
     partner_copy().wait_recv()
     for j in range(height // TS):
@@ -341,9 +322,10 @@
     def _():
         t_copy().start()
 
+    ring_next(0, 1)
+
     loop(chips - 1, lambda i: z_copy(i).wait_recv())
     share_copy().start()
-    ring_next(0, 1)
     share_copy().wait_recv()
     flat = jnp.transpose(
         jnp.concatenate([zbuf[i % 2, i // 2] for i in range(rows)], axis=0))
@@ -371,7 +353,7 @@
     def _():
         t_copy().wait_recv()
 
-    ring_start(1, 0)
+    ring_next(1, 0)
     ring_next(0, 2)
 
     listed = jnp.transpose(jnp.broadcast_to(map_lanes[...].astype(F32), (128, 128)))
@@ -390,9 +372,6 @@
     flag_p = spread(lambda lane: 4 * lax.shift_right_logical(lane, 3), PW)[0:1]
     flags[0:8, :height] = spread(lambda lane: 4 * r + lax.shift_right_logical(lane, 7), height).astype(F32)
     flags[0:8, height:] = spread(lambda lane: 8 * c + lax.shift_right_logical(lane, 7), width).astype(F32)
-
-    ring_next(0, 3)
-    ring_next(1, 0)
 
     loop(cols - 1, lambda i: vp_copy(i).wait_recv())
     for k in range(2):
@@ -404,50 +383,39 @@
     eye = jnp.where(i == j, 1.0, 0.0).astype(F32)
     work[:, :PW] = dot1(wp[0], wp[0], 0, 0)
     work[:, PW:] = eye
-    ring_next(0, 4)
+    ring_next(0, 3)
     ring_next(1, 1)
     loop(cols - 1, lambda i: d_copy(i).wait_recv())
     work[:, :PW] += diag[0]
 
     def beside(t):
-        @pl.when(t == 1)
-        def _():
-            ring_next(0, 5)
+        if t == 2:
             ring_next(1, 2)
-
-        @pl.when(t == 3)
-        def _():
-            ring_next(0, 6)
+        if t == 3:
+            ring_next(0, 4)
+        if t == 5:
             ring_next(1, 3)
-
-        @pl.when(t == 5)
-        def _():
-            ring_next(0, 7)
-            ring_next(1, 4)
             loop(cols - 1, lambda i: d1_copy(i).wait_recv())
             d1_share().start()
 
-        @pl.when(t == 7)
-        def _():
-            ring_next(1, 5)
-
-    loop(PW // NB, lambda b: factor_step(work, b, beside, lambda b: None))
+    for b in range(PW // NB):
+        factor_step(work, b, beside, lambda b: None)
     x0[...] = left3(work[:, PW:])
     d1_share().wait_recv()
-    ring_next(1, 6)
+    ring_next(1, 4)
     low = diag[1] + dot1(wp[1], wp[0], 0, 0)
     p01[...] = dot1(right3(low, 1), x0[...], 1, 1).astype(BF16)
 
     work[:, :PW] = diag[2] + dot1(wp[1], wp[1], 0, 0) - dot1(p01[...], p01[...], 1, 1)
     work[:, PW:] = eye
 
-    def first_part(strip, v, flag, at):
+    def first_part(strip0, strip1, v, flag):
         flag = flag.astype(BF16)
         bottom = v * flag
         w = jnp.concatenate([v - bottom, bottom], axis=0)
-        s0 = strip[0, :, at] + dot1(wp[0], w, 0, 0)
+        s0 = strip0 + dot1(wp[0], w, 0, 0)
         first = dot1(x0[...], right3(s0, 0), 1, 0).astype(BF16)
-        s1 = strip[1, :, at] + dot1(wp[1], w, 0, 0) - dot1(p01[...], first, 1, 0)
+        s1 = strip1 + dot1(wp[1], w, 0, 0) - dot1(p01[...], first, 1, 0)
         return w, first, right3(s1, 0)
 
     def col_tile(q, h):
@@ -455,7 +423,9 @@
         at = slice(q * height + h * PW, q * height + (h + 1) * PW)
         v = jnp.concatenate([v_c[2 * i + q, :, sub] for i in range(chips)], axis=0)
         flag = flags[0:1, height + at.start : height + at.stop]
-        w, first, rest = first_part(strip_c, v, flag, at)
+        strip = strip_c[:, :, at].astype(F32)
+        w, first, rest = first_part(
+            strip[:, :8].reshape(PW, PW), strip[:, 8:].reshape(PW, PW), v, flag)
         out_b[0 : 2 * PW, at] = w
         out_b[2 * PW : 3 * PW, at] = -first
         later[:, at] = rest
@@ -464,7 +434,6 @@
 
     def beside_second(t):
         if t == 2:
-            ring_next(1, 7)
             for a in range(2):
                 loop(chips, lambda i: sib_copy(a, 2 * i + core).wait_recv())
 
@@ -488,7 +457,8 @@
         loop(cols - 1, lambda i: copy(i).wait_recv())
     for h in range(height // PW):
         at = slice(h * PW, (h + 1) * PW)
-        w, first, rest = first_part(strip_r, v_r[:, at], flags[0:1, at], at)
+        w, first, rest = first_part(
+            strip_r[0, :, at], strip_r[1, :, at], v_r[:, at], flags[0:1, at])
         second = dot1(x1[...], rest, 1, 0).astype(BF16)
         turned_r[0:PW, at] = first
         turned_r[PW:, at] = second
@@ -511,8 +481,9 @@
         loop(cols - 1, lambda i: copy(i).wait_send())
     for a in range(2):
         loop(chips, lambda i: sib_copy(a, 2 * i + core).wait_send())
-        loop(hops, lambda s: ring_copy(a, 0, s).wait_send())
-        loop(hops - 1, lambda s: ring_copy(a, 1, s).wait_send())
+        for stage in range(hops // 2):
+            for way, d in ring_pairs(stage):
+                ring_copy(a, way, d).wait_send()
 
 
 def panels(front, child, tile_group, row_map, rows, cols):
@@ -544,7 +515,7 @@
             pltpu.VMEM((3, PW, PW), F32),
             pltpu.VMEM((2, PW, PW), BF16),
             pltpu.VMEM((2, PW, height), F32),
-            pltpu.VMEM((2, PW, width), F32),
+            pltpu.VMEM((rows, 16, width), BF16),
             pltpu.VMEM((PW, height), BF16),
             pltpu.VMEM((rows, 16, height), BF16),
             pltpu.VMEM((8, height + width), F32),

time: 87.5 us -> 77.8 us (0.89)
  the two profiles are of different devices: /device:TPU:6 before, /device:TPU:36 now
where the time goes in v5:
time: 77.8 us; the launch traced here: 77.7 us
  Pallas kernels  76.8 us (99%)
  between operations  0.83 us (1%)
    pallas_call x1, Pallas kernels, panels(): pl.pallas_call(front_kernel, out_shape=(shape((height, 4 * PW), BF16), sh...  73.4 us
    pallas_call x1, Pallas kernels, final(): pl.pallas_call(final_kernel, out_shape=(jax.ShapeDtypeStruct((rows, width...  3.47 us

profile of v5, /device:TPU:36, one launch (start us, length us, event | category | flops | bytes accessed | tf_op | source)
XLA Modules:
  0.0 77.7 jit_solution(10218453538645821220)
XLA Ops:
  0.6 0.0 copy-start.1
  0.6 0.0 copy-start
  0.7 73.4 %shard_map.59 = (bf16[512,1024]{1,0:T(8,128)(2,1)S(1)}, bf16[1024,1024]{1,0:T(8,128)(2,1)S(1)}, bf16[32,512]{1,0:T(8,128)(2,1)S(1)}) custom-call(f32[512,1024]{1,0:T(8,128)} %front.1, bf16[16,512]{1,0:T(8,128)(2,1)} %bitcast.3, s32[32]{0:T(128)} %groups.1, s32[128]{0:T(128)} %map_hbm.1, s32[1,128]{1,0:T(1,128)} %bitcast.4), custom_call_target="tpu_custom_call" | custom-call | tf_op jit(solution)/shard_map/pallas_call | solution.py:494
  74.0 0.0 copy-done.1
  74.0 0.0 copy-done
  74.0 3.5 %shard_map.60 = (f32[512,1024]{1,0:T(8,128)}, bf16[32,512]{1,0:T(8,128)(2,1)}) custom-call(f32[512,1024]{1,0:T(8,128)S(1)} %copy-done, bf16[512,1024]{1,0:T(8,128)(2,1)S(1)} %get-tuple-element.7.left, bf16[1024,1024]{1,0:T(8,128)(2,1)S(1)} %get-tuple-element.8.right, bf16[32,512]{1,0:T(8,128)(2,1)S(1)} %get-tuple-element.9.own_p, s32[32]{0:T(128)S(1)} %copy-done.1), custom_call_target="tpu_custom_call" | custom-call | tf_op jit(solution)/shard_map/pallas_call | solution.py:574
Async XLA Ops:
  0.6 73.4 %copy-start.1 = (s32[32]{0:T(128)S(1)}, s32[32]{0:T(128)}, u32[]{:S(2)}) copy-start(s32[32]{0:T(128)} %groups.1) | copy-start | bytes 388
  0.6 73.4 %copy-start = (f32[512,1024]{1,0:T(8,128)S(1)}, f32[512,1024]{1,0:T(8,128)}, u32[]{:S(2)}) copy-start(f32[512,1024]{1,0:T(8,128)} %front.1) | copy-start | bytes 6291460

commit v6 on v5

--- a/solution.py
+++ b/solution.py
@@ -54,35 +54,26 @@
         m.append(jnp.where(ll < NB, block[8 * g : 8 * g + 8, :], unit))
     for g in range(groups):
         low = 8 * g
-        rest = range(g + 1, groups)
         rows = [jnp.broadcast_to(m[g][i : i + 1, :], (8, 128)) for i in range(8)]
-        s = {}
-        for i in range(8):
-            for k in range(i, 8):
-                s[i, k] = jnp.broadcast_to(rows[i][:, low + k : low + k + 1], (8, 128))
         cols = {}
-        for h in rest:
+        for h in range(g, groups):
             for k in range(8):
                 cols[h, k] = jnp.broadcast_to(m[h][:, low + k : low + k + 1], (8, 128))
         for j in range(8):
-            inv = lax.rsqrt(s[j, j])
+            inv = lax.rsqrt(jnp.broadcast_to(cols[g, j][j : j + 1, :], (8, 128)))
+            rows[j] = rows[j] * inv
+            for h in range(g, groups):
+                cols[h, j] = cols[h, j] * inv
             for k in range(j + 1, 8):
-                s[j, k] = s[j, k] * inv
-            for i in range(j + 1, 8):
-                for k in range(i, 8):
-                    s[i, k] = s[i, k] - s[j, i] * s[j, k]
-            rows[j] = rows[j] * inv
-            for i in range(j + 1, 8):
-                rows[i] = rows[i] - s[j, i] * rows[j]
-            for h in rest:
-                cols[h, j] = cols[h, j] * inv
-                for i in range(j + 1, 8):
-                    cols[h, i] = cols[h, i] - s[j, i] * cols[h, j]
+                factor = jnp.broadcast_to(cols[g, j][k : k + 1, :], (8, 128))
+                for h in range(g, groups):
+                    cols[h, k] = cols[h, k] - factor * cols[h, j]
+                rows[k] = rows[k] - factor * rows[j]
         merged = rows[0]
         for i in range(1, 8):
             merged = jnp.where(ii == i, rows[i], merged)
         m[g] = merged
-        for h in rest:
+        for h in range(g + 1, groups):
             for j in range(8):
                 m[h] = m[h] - cols[h, j] * rows[j]
     return jnp.concatenate(m, axis=0)[:, NB : 2 * NB]
@@ -290,7 +281,17 @@
 
     def d1_share():
         return pltpu.make_async_remote_copy(
-            src_ref=diag.at[1 + core], dst_ref=diag.at[1 + core], send_sem=d_s, recv_sem=d_r,
+            src_ref=diag.at[1 + core], dst_ref=diag.at[1 + core], send_sem=d_s.at[0], recv_sem=d_r.at[0],
+            device_id=(2 * z + 1 - core, c), device_id_type=MESH)
+
+    def d_share():
+        return pltpu.make_async_remote_copy(
+            src_ref=diag.at[0], dst_ref=diag.at[0], send_sem=d_s.at[1], recv_sem=d_r.at[1],
+            device_id=(2 * z + 1 - core, c), device_id_type=MESH)
+
+    def vp_share():
+        return pltpu.make_async_remote_copy(
+            src_ref=vpiv, dst_ref=vpiv, send_sem=d_s.at[2], recv_sem=d_r.at[2],
             device_id=(2 * z + 1 - core, c), device_id_type=MESH)
 
     def vp_copy(i):
@@ -339,11 +340,18 @@
 
     vpiece[0] = (flat[64:80] + swapped_halves(flat[80:96])).astype(BF16)
     vpiece[1] = (flat[96:112] + swapped_halves(flat[112:128])).astype(BF16)
-    diag[0, own16, :] = dpiece[0]
     diag[1 + core, own16, :] = dpiece[1 + core]
-    vpiv[:, own16, :] = vpiece[...]
-    loop(cols - 1, lambda i: vp_copy(i).start())
-    loop(cols - 1, lambda i: d_copy(i).start())
+
+    @pl.when(core == 0)
+    def _():
+        diag[0, own16, :] = dpiece[0]
+        loop(cols - 1, lambda i: d_copy(i).start())
+
+    @pl.when(core == 1)
+    def _():
+        vpiv[:, own16, :] = vpiece[...]
+        loop(cols - 1, lambda i: vp_copy(i).start())
+
     loop(cols - 1, lambda i: d1_copy(i).start())
 
     loop(cols - 1, lambda i: vr_copy(i).start())
@@ -373,7 +381,21 @@
     flags[0:8, :height] = spread(lambda lane: 4 * r + lax.shift_right_logical(lane, 7), height).astype(F32)
     flags[0:8, height:] = spread(lambda lane: 8 * c + lax.shift_right_logical(lane, 7), width).astype(F32)
 
-    loop(cols - 1, lambda i: vp_copy(i).wait_recv())
+    ring_next(0, 3)
+    ring_next(1, 1)
+
+    @pl.when(core == 0)
+    def _():
+        loop(cols - 1, lambda i: d_copy(i).wait_recv())
+        d_share().start()
+        vp_share().wait_recv()
+
+    @pl.when(core == 1)
+    def _():
+        loop(cols - 1, lambda i: vp_copy(i).wait_recv())
+        vp_share().start()
+        d_share().wait_recv()
+
     for k in range(2):
         vp = vpiv[k]
         wp[k, PW:, :] = vp * flag_p
@@ -381,12 +403,8 @@
     i = lax.broadcasted_iota(jnp.int32, (PW, PW), 0)
     j = lax.broadcasted_iota(jnp.int32, (PW, PW), 1)
     eye = jnp.where(i == j, 1.0, 0.0).astype(F32)
-    work[:, :PW] = dot1(wp[0], wp[0], 0, 0)
+    work[:, :PW] = diag[0] + dot1(wp[0], wp[0], 0, 0)
     work[:, PW:] = eye
-    ring_next(0, 3)
-    ring_next(1, 1)
-    loop(cols - 1, lambda i: d_copy(i).wait_recv())
-    work[:, :PW] += diag[0]
 
     def beside(t):
         if t == 2:
@@ -477,7 +495,17 @@
     def _():
         t_copy().wait_send()
 
-    for copy in (sr_copy, d_copy, d1_copy, vp_copy, vr_copy):
+    @pl.when(core == 0)
+    def _():
+        d_share().wait_send()
+        loop(cols - 1, lambda i: d_copy(i).wait_send())
+
+    @pl.when(core == 1)
+    def _():
+        vp_share().wait_send()
+        loop(cols - 1, lambda i: vp_copy(i).wait_send())
+
+    for copy in (sr_copy, d1_copy, vr_copy):
         loop(cols - 1, lambda i: copy(i).wait_send())
     for a in range(2):
         loop(chips, lambda i: sib_copy(a, 2 * i + core).wait_send())
@@ -529,7 +557,7 @@
             dma((rows // 2,)), dma((rows // 2,)), dma, dma, dma, dma,
             dma((5, cols - 1)), dma((5, cols - 1)),
             dma((2, 2, rows // 4)), dma((2, 2, rows // 4)),
-            dma((2, rows // 2)), dma((2, rows // 2)), dma, dma,
+            dma((2, rows // 2)), dma((2, rows // 2)), dma((3,)), dma((3,)),
         ],
         compiler_params=pltpu.CompilerParams(
             collective_id=0, has_side_effects=True, vmem_limit_bytes=40 << 20),

time: 77.8 us -> 76.3 us (0.981)
  Pallas kernels: 76.8 us -> 75.3 us
    pallas_call x1, Pallas kernels: 73.4 us -> 71.9 us  [panels(): pl.pallas_call(front_kernel, out_shape=(shape((height, 4 * PW), BF16), sh...]
where the time goes in v6:
time: 76.3 us; the launch traced here: 76.2 us
  Pallas kernels  75.3 us (99%)
  between operations  0.83 us (1%)
    pallas_call x1, Pallas kernels, panels(): pl.pallas_call(front_kernel, out_shape=(shape((height, 4 * PW), BF16), sh...  71.9 us
    pallas_call x1, Pallas kernels, final(): pl.pallas_call(final_kernel, out_shape=(jax.ShapeDtypeStruct((rows, width...  3.48 us

profile of v6, /device:TPU:36, one launch (start us, length us, event | category | flops | bytes accessed | tf_op | source)
XLA Modules:
  0.0 76.2 jit_solution(909397598794398517)
XLA Ops:
  0.6 0.0 copy-start.1
  0.6 0.0 copy-start
  0.7 71.9 %shard_map.59 = (bf16[512,1024]{1,0:T(8,128)(2,1)S(1)}, bf16[1024,1024]{1,0:T(8,128)(2,1)S(1)}, bf16[32,512]{1,0:T(8,128)(2,1)S(1)}) custom-call(f32[512,1024]{1,0:T(8,128)} %front.1, bf16[16,512]{1,0:T(8,128)(2,1)} %bitcast.3, s32[32]{0:T(128)} %groups.1, s32[128]{0:T(128)} %map_hbm.1, s32[1,128]{1,0:T(1,128)} %bitcast.4), custom_call_target="tpu_custom_call" | custom-call | tf_op jit(solution)/shard_map/pallas_call | solution.py:522
  72.5 0.0 copy-done.1
  72.5 0.0 copy-done
  72.6 3.5 %shard_map.60 = (f32[512,1024]{1,0:T(8,128)}, bf16[32,512]{1,0:T(8,128)(2,1)}) custom-call(f32[512,1024]{1,0:T(8,128)S(1)} %copy-done, bf16[512,1024]{1,0:T(8,128)(2,1)S(1)} %get-tuple-element.7.left, bf16[1024,1024]{1,0:T(8,128)(2,1)S(1)} %get-tuple-element.8.right, bf16[32,512]{1,0:T(8,128)(2,1)S(1)} %get-tuple-element.9.own_p, s32[32]{0:T(128)S(1)} %copy-done.1), custom_call_target="tpu_custom_call" | custom-call | tf_op jit(solution)/shard_map/pallas_call | solution.py:602
Async XLA Ops:
  0.6 71.9 %copy-start.1 = (s32[32]{0:T(128)S(1)}, s32[32]{0:T(128)}, u32[]{:S(2)}) copy-start(s32[32]{0:T(128)} %groups.1) | copy-start | bytes 388
  0.6 71.9 %copy-start = (f32[512,1024]{1,0:T(8,128)S(1)}, f32[512,1024]{1,0:T(8,128)}, u32[]{:S(2)}) copy-start(f32[512,1024]{1,0:T(8,128)} %front.1) | copy-start | bytes 6291460

commit v7 on v6

--- a/solution.py
+++ b/solution.py
@@ -381,9 +381,6 @@
     flags[0:8, :height] = spread(lambda lane: 4 * r + lax.shift_right_logical(lane, 7), height).astype(F32)
     flags[0:8, height:] = spread(lambda lane: 8 * c + lax.shift_right_logical(lane, 7), width).astype(F32)
 
-    ring_next(0, 3)
-    ring_next(1, 1)
-
     @pl.when(core == 0)
     def _():
         loop(cols - 1, lambda i: d_copy(i).wait_recv())
@@ -407,12 +404,16 @@
     work[:, PW:] = eye
 
     def beside(t):
-        if t == 2:
+        if t == 0:
+            ring_next(0, 3)
+            ring_next(1, 1)
+        if t == 3:
             ring_next(1, 2)
-        if t == 3:
+        if t == 4:
             ring_next(0, 4)
+        if t == 6:
+            ring_next(1, 3)
         if t == 5:
-            ring_next(1, 3)
             loop(cols - 1, lambda i: d1_copy(i).wait_recv())
             d1_share().start()
 
@@ -420,7 +421,6 @@
         factor_step(work, b, beside, lambda b: None)
     x0[...] = left3(work[:, PW:])
     d1_share().wait_recv()
-    ring_next(1, 4)
     low = diag[1] + dot1(wp[1], wp[0], 0, 0)
     p01[...] = dot1(right3(low, 1), x0[...], 1, 1).astype(BF16)
 
@@ -451,7 +451,9 @@
     tiles = [(q, h) for q in range(2) for h in range(height // PW)]
 
     def beside_second(t):
-        if t == 2:
+        if t == 1:
+            ring_next(1, 4)
+        if t == 4:
             for a in range(2):
                 loop(chips, lambda i: sib_copy(a, 2 * i + core).wait_recv())
 

time: 76.3 us -> 77.6 us (1.017)
  the two profiles are of different devices: /device:TPU:36 before, /device:TPU:6 now
where the time goes in v7:
time: 77.6 us; the launch traced here: 76.8 us
  Pallas kernels  76 us (98%)
  between operations  0.83 us (1%)
    pallas_call x1, Pallas kernels, panels(): pl.pallas_call(front_kernel, out_shape=(shape((height, 4 * PW), BF16), sh...  72.5 us
    pallas_call x1, Pallas kernels, final(): pl.pallas_call(final_kernel, out_shape=(jax.ShapeDtypeStruct((rows, width...  3.48 us

profile of v7, /device:TPU:6, one launch (start us, length us, event | category | flops | bytes accessed | tf_op | source)
XLA Modules:
  0.0 76.8 jit_solution(16042058880528355588)
XLA Ops:
  0.6 0.0 copy-start.1
  0.6 0.0 copy-start
  0.7 72.5 %shard_map.59 = (bf16[512,1024]{1,0:T(8,128)(2,1)S(1)}, bf16[1024,1024]{1,0:T(8,128)(2,1)S(1)}, bf16[32,512]{1,0:T(8,128)(2,1)S(1)}) custom-call(f32[512,1024]{1,0:T(8,128)} %front.1, bf16[16,512]{1,0:T(8,128)(2,1)} %bitcast.3, s32[32]{0:T(128)} %groups.1, s32[128]{0:T(128)} %map_hbm.1, s32[1,128]{1,0:T(1,128)} %bitcast.4), custom_call_target="tpu_custom_call" | custom-call | tf_op jit(solution)/shard_map/pallas_call | solution.py:524
  73.2 0.0 copy-done.1
  73.2 0.0 copy-done
  73.2 3.5 %shard_map.60 = (f32[512,1024]{1,0:T(8,128)}, bf16[32,512]{1,0:T(8,128)(2,1)}) custom-call(f32[512,1024]{1,0:T(8,128)S(1)} %copy-done, bf16[512,1024]{1,0:T(8,128)(2,1)S(1)} %get-tuple-element.7.left, bf16[1024,1024]{1,0:T(8,128)(2,1)S(1)} %get-tuple-element.8.right, bf16[32,512]{1,0:T(8,128)(2,1)S(1)} %get-tuple-element.9.own_p, s32[32]{0:T(128)S(1)} %copy-done.1), custom_call_target="tpu_custom_call" | custom-call | tf_op jit(solution)/shard_map/pallas_call | solution.py:604
Async XLA Ops:
  0.6 72.5 %copy-start.1 = (s32[32]{0:T(128)S(1)}, s32[32]{0:T(128)}, u32[]{:S(2)}) copy-start(s32[32]{0:T(128)} %groups.1) | copy-start | bytes 388
  0.6 72.5 %copy-start = (f32[512,1024]{1,0:T(8,128)S(1)}, f32[512,1024]{1,0:T(8,128)}, u32[]{:S(2)}) copy-start(f32[512,1024]{1,0:T(8,128)} %front.1) | copy-start | bytes 6291460
